TPU v7x, 256 devices: a whole 4x4x8 slice. The times are simulated.
256 devices in a mesh: gx: 32 (over z_hi, x, core), gy: 8 (over y, z_lo).
Axes of the slice: x: 4, y: 4, z: 8 (z_hi: 4, z_lo: 2; z = z_hi * 2 + z_lo), core: 2. Of those that a mesh axis runs over, the one named last changes fastest.
Arguments:
- populations: float32 [19, 16, 512, 1024], P(None, None, 'gx', 'gy'), as said below
- solid_mask: int32 [16, 512, 1024], P(None, 'gx', 'gy'), may hold values 0 or 1
- bead_states: float32 [32, 8, 8, 9, 1280], P('gx', 'gy'), as said below
- bead_bricks: int32 [32, 8, 8, 20], P('gx', 'gy'), may hold values from 0 to 63, as said below
- leave_dir: int32 [32, 8, 8], P('gx', 'gy'), may hold values from 0 to 4, as said below
- stiffness: bfloat16 [1280, 1280], replicated, may hold values from -0.15625 to 0.15625
Outputs:
- populations_out: float32 [19, 16, 512, 1024], P(None, None, 'gx', 'gy')
- vertex_out: float32 [32, 8, 16, 9, 1280], P('gx', 'gy')
Inputs may be any that keep to these rules, and one draw needn't show every extreme that they name: `populations`: every entry is positive. `bead_states`: in the second dimension from the end, entries 0 to 2 are a vertex's x, y, z cell coordinates inside its block's brick, from 1 to 6; entries 3 to 5 its displacement from the reference shape; entries 6 to 8 its velocity. Every slot holds a bead. `bead_bricks`: a brick index counted in the tile that holds the bead after migration. `leave_dir`: 0 keeps the bead on its tile; 1 and 2 move it to the next tile along +x and -x, 3 and 4 along +y and -y. On every tile at most 2 beads have any one code from 1 to 4, and exactly 2 have one of them.
All inputs are finite; a program needn't handle non-finite values. No bound on the sum of `solid_mask` on one device may be relied on, other than what follows from the above.
Results may differ from a plain program's by a relative error of at most 0.00036.
Values sent between devices are 32-bit elements; how exact they have to be, the bound alone decides.
No kernel may reach another device: no remote copies, remote signals or barrier semaphores. Data moves between devices by JAX's collectives and lax.ppermute only.
A program may use at most 128 MiB of HBM per device.

v0:
```python
import functools

import jax
import jax.numpy as jnp
import numpy as np
from jax import lax
from jax.experimental import pallas as pl
from jax.experimental.pallas import tpu as pltpu
from jax.sharding import PartitionSpec as P

LATTICE = [
    (0, 0, 0),
    (1, 0, 0),
    (-1, 0, 0),
    (0, 1, 0),
    (0, -1, 0),
    (0, 0, 1),
    (0, 0, -1),
    (1, 1, 0),
    (-1, -1, 0),
    (1, -1, 0),
    (-1, 1, 0),
    (1, 0, 1),
    (-1, 0, -1),
    (1, 0, -1),
    (-1, 0, 1),
    (0, 1, 1),
    (0, -1, -1),
    (0, 1, -1),
    (0, -1, 1),
]
WEIGHTS = [1.0 / 3.0] + [1.0 / 18.0] * 6 + [1.0 / 36.0] * 12
X_UP = [1, 7, 9, 11, 13]
X_DOWN = [2, 8, 10, 12, 14]
Y_UP = [3, 7, 10, 15, 17]
Y_DOWN = [4, 8, 9, 16, 18]
CORNERS = [(7, 1, 1), (8, -1, -1), (9, 1, -1), (10, -1, 1)]

NZ, CX, CY = 16, 16, 128
SLOTS, SIDES, MIG, ALL = 8, 4, 2, 16
VERT, BLOCKS, CHUNK = 1280, 20, 256
F32, BF16 = jnp.float32, jnp.bfloat16


def lanes(shape):
    return lax.broadcasted_iota(jnp.int32, shape, len(shape) - 1)


def rows(shape):
    return lax.broadcasted_iota(jnp.int32, shape, len(shape) - 2)


def pack_kernel(leave, bricks, pops, states, *outs):
    faces, corners = outs[:4], outs[4:]
    lane = lanes((CX, CY))
    for side in range(4):
        out = faces[side]
        first, second, count = jnp.int32(0), jnp.int32(0), jnp.int32(0)
        for slot in range(SLOTS):
            hit = leave[0, 0, slot] == side + 1
            first = jnp.where(hit & (count == 0), slot, first)
            second = jnp.where(hit & (count == 1), slot, second)
            count = count + hit.astype(jnp.int32)
        for place, slot in enumerate((first, second)):
            out[8 * place : 8 * place + 8, :] = states[0, 0, slot, 0:8, :]
            out[16 + place : 17 + place, :] = states[0, 0, slot, 8:9, :]
            valid = (count > place).astype(F32)
            out[18 + place : 19 + place, 0:128] = jnp.full((1, 128), 1.0, F32) * valid
            out[18 + place : 19 + place, 0:BLOCKS] = bricks[0, 0, pl.ds(slot, 1), :].astype(F32)
    for side, (group, x) in enumerate(((X_UP, CX - 1), (X_DOWN, 0))):
        for i, q in enumerate(group):
            face = pops[q, pl.ds(x, NZ, stride=CX), :]
            for half in range(2):
                at = (half * 5 + i) * CY
                faces[side][24:32, at : at + CY] = face[8 * half : 8 * half + 8]
    columns = []
    for side, (group, y) in enumerate(((Y_UP, CY - 1), (Y_DOWN, 0))):
        column = jnp.zeros((CX, CY), F32)
        for i, q in enumerate(group):
            for z in range(NZ):
                plane = pops[q, z * CX : (z + 1) * CX, :]
                place = i * NZ + z
                column = jnp.where(lane == place, pltpu.roll(plane, (place - y) % CY, 1), column)
        faces[2 + side][24:32, 0:CY] = column[0:8]
        faces[2 + side][24:32, CY : 2 * CY] = column[8:16]
        columns.append(column)
    for out, (_, dx, dy) in zip(corners, CORNERS):
        column = columns[0 if dy > 0 else 1]
        out[...] = column[8:16] if dx > 0 else column[0:8]


def pack(leave, bricks, pops, states):
    vmem = pl.BlockSpec(memory_space=pltpu.VMEM)
    return pl.pallas_call(
        pack_kernel,
        out_shape=[jax.ShapeDtypeStruct((32, VERT), F32)] * 4
        + [jax.ShapeDtypeStruct((8, 128), F32)] * 4,
        in_specs=[pl.BlockSpec(memory_space=pltpu.SMEM), vmem, vmem, vmem],
        out_specs=[vmem] * 8,
        compiler_params=pltpu.CompilerParams(vmem_limit_bytes=32 << 20),
        name="pack_messages",
    )(leave, bricks, pops, states)


def phi(distance):
    t = distance * distance
    value = jnp.full(t.shape, COSINE[-1], F32)
    for coefficient in COSINE[-2::-1]:
        value = value * t + coefficient
    return jnp.where(jnp.abs(distance) < 2.0, 0.5 * (value * value), 0.0)


def cosine_terms():
    terms, term = [], 1.0
    for n in range(8):
        terms.append(float(term))
        term = -term * (np.pi / 4) ** 2 / ((2 * n + 1) * (2 * n + 2))
    return terms


COSINE = cosine_terms()


def step_kernel(
    leave, bricks, pops, solid, states,
    x_low, x_high, y_low, y_high, c_pp, c_mm, c_pm, c_mp,
    stiffness,
    pops_out, vertex_out,
    read, flow, halo_x, halo_y, turn, cells, force, moved, last, push, weights,
    meta, order, meta_sem, out_sem,
):
    faces = (x_low, x_high, y_low, y_high)
    copies = [
        pltpu.make_async_copy(faces[side].at[16:24, 0:128], meta.at[side], meta_sem.at[side])
        for side in range(4)
    ]
    for copy in copies:
        copy.start()

    for side in range(2):
        for i in range(5):
            for half in range(2):
                at = (half * 5 + i) * CY
                halo_x[side * 5 + i, 8 * half : 8 * half + 8, :] = faces[side][24:32, at : at + CY]
    row16 = rows((CX, CY))
    lane16 = lanes((CX, CY))
    corner = {7: (c_pp, 7), 8: (c_mm, 0), 9: (c_pm, 7), 10: (c_mp, 0)}
    for side, group in enumerate((Y_UP, Y_DOWN)):
        column = jnp.concatenate(
            [faces[2 + side][24:32, 0:CY], faces[2 + side][24:32, CY : 2 * CY]], axis=0
        )
        for i, q in enumerate(group):
            cx = LATTICE[q][0]
            if cx == 0:
                halo_y[side * 5 + i] = column
            else:
                source, row = corner[q]
                edge = jnp.broadcast_to(source[row : row + 1, :], (CX, CY))
                moved_column = pltpu.roll(column, cx % CX, 0)
                halo_y[side * 5 + i] = jnp.where(
                    row16 == (0 if cx > 0 else CX - 1), edge, moved_column
                )

    def pull(z, carry):
        density = None
        momentum = [None, None, None]
        at = pl.ds(pl.multiple_of(z * CX, CX), CX)
        for q in range(19):
            cx, cy, cz = LATTICE[q]
            source = (z - cz) & (NZ - 1)
            value = pops[q, pl.ds(pl.multiple_of(source * CX, CX), CX), :]
            if cx != 0:
                side, group = (0, X_UP) if cx > 0 else (1, X_DOWN)
                edge = halo_x[side * 5 + group.index(q), pl.ds(source, 1), :]
                value = jnp.where(
                    row16 == (0 if cx > 0 else CX - 1),
                    jnp.broadcast_to(edge, (CX, CY)),
                    pltpu.roll(value, cx % CX, 0),
                )
            if cy != 0:
                side, group = (0, Y_UP) if cy > 0 else (1, Y_DOWN)
                i = group.index(q)
                y = 0 if cy > 0 else CY - 1
                column = pltpu.roll(
                    halo_y[side * 5 + i], (y + 2 * CY - i * NZ - source) & (CY - 1), 1
                )
                value = jnp.where(lane16 == y, column, pltpu.roll(value, cy % CY, 1))
            read[q, at, :] = value
            density = value if density is None else density + value
            for k, c in enumerate((cx, cy, cz)):
                if c != 0:
                    signed = value if c > 0 else -value
                    momentum[k] = signed if momentum[k] is None else momentum[k] + signed
        inverse = 1.0 / density
        flow[0, at, :] = density
        for k in range(3):
            flow[1 + k, at, :] = momentum[k]
            flow[4 + k, at, :] = momentum[k] * inverse
        return carry

    lax.fori_loop(0, NZ, pull, 0)

    left = lanes((16, 128)) < 64
    for k in range(3):
        for bz in range(2):
            tiles = [
                flow[4 + k, (8 * bz + iz) * CX + 8 * bx : (8 * bz + iz) * CX + 8 * bx + 8, :]
                for bx in range(2)
                for iz in range(8)
            ]
            turn[...] = jnp.concatenate(tiles, axis=0).T
            for j in range(4):
                even = turn[pl.ds(2 * j, 16, stride=8), :]
                odd = turn[pl.ds(2 * j + 1, 16, stride=8), :]
                pairs = (
                    jnp.where(left, even, pltpu.roll(odd, 64, 1)),
                    jnp.where(left, pltpu.roll(even, 64, 1), odd),
                )
                for bx in range(2):
                    base = (bz * 2 + bx) * 16 * 8
                    cells[j, pl.ds(base + k, 16, stride=8), :] = pairs[bx]
                    cells[j, pl.ds(base + 3 + k, 16, stride=8), :] = pairs[bx]
                    if k < 2:
                        cells[j, pl.ds(base + 6 + k, 16, stride=8), :] = pairs[bx]

    for slot in range(SLOTS):
        moved[slot] = states[0, 0, slot, 0:8, :]
        last[slot : slot + 1, :] = states[0, 0, slot, 8:9, :]
    for side in range(4):
        for place in range(MIG):
            slot = SLOTS + side * MIG + place
            moved[slot] = faces[side][8 * place : 8 * place + 8, :]
            last[slot : slot + 1, :] = faces[side][16 + place : 17 + place, :]

    shape = moved[...].reshape(ALL * 8, VERT).astype(BF16)
    for n in range(5):
        at = slice(n * 256, (n + 1) * 256)
        push[:, at] = -jnp.dot(shape, stiffness[:, at], preferred_element_type=F32)

    force[...] = jnp.zeros(force.shape, F32)
    vertex_out[...] = jnp.zeros(vertex_out.shape, F32)

    for copy in copies:
        copy.wait()
    count = jnp.int32(0)
    for slot in range(SLOTS):
        order[count] = slot
        count = count + (leave[0, 0, slot] == 0).astype(jnp.int32)
    for side in range(4):
        for place in range(MIG):
            order[count] = SLOTS + side * MIG + place
            count = count + (meta[side, 2 + place, 64] > 0.5).astype(jnp.int32)

    row8 = rows((8, CHUNK))
    step8 = row8.astype(F32)
    lane8 = lanes((8, CHUNK))
    third = row8 % 3

    def couple(turn_number, carry):
        slot = order[turn_number]
        guest = jnp.maximum(slot - SLOTS, 0)
        for chunk in range(VERT // CHUNK):
            at = slice(chunk * CHUNK, (chunk + 1) * CHUNK)
            table = weights.at[chunk % 2]
            bead = moved[slot, :, at]
            along = [
                phi(jnp.broadcast_to(bead[k : k + 1, :], (8, CHUNK)) - step8) for k in range(3)
            ]
            along_x, along_y, along_z = along
            planes = [
                jnp.broadcast_to(along_z[iz : iz + 1, :], (8, CHUNK)) * along_x for iz in range(8)
            ]
            for iy in range(8):
                factor = jnp.broadcast_to(along_y[iy : iy + 1, :], (8, CHUNK))
                for pair in range(4):
                    both = jnp.concatenate(
                        [planes[2 * pair] * factor, planes[2 * pair + 1] * factor], axis=0
                    )
                    first = iy * 64 + pair * 16
                    table[first : first + 16, :] = both.astype(BF16)
            homes = []
            for b in range(CHUNK // 64):
                block = chunk * (CHUNK // 64) + b
                mine = bricks[0, 0, jnp.minimum(slot, SLOTS - 1), block]
                theirs = meta[guest // 2, 2 + guest % 2, block].astype(jnp.int32)
                homes.append(pl.multiple_of(jnp.where(slot < SLOTS, mine, theirs) * 8, 8))
            nearby = jnp.concatenate(
                [
                    jnp.concatenate([cells[j, pl.ds(home, 8), :] for j in range(4)], axis=1)
                    for home in homes
                ],
                axis=0,
            ).astype(BF16)
            drive = push[pl.ds(pl.multiple_of(slot * 8, 8), 8), at]
            drives = jnp.concatenate(
                [jnp.where(lane8 // 64 == b, drive, 0.0) for b in range(CHUNK // 64)], axis=0
            ).astype(BF16)
            sampled = jnp.dot(nearby, table[...], preferred_element_type=F32)
            spread = lax.dot_general(
                drives, table[...], (((1,), (1,)), ((), ())), preferred_element_type=F32
            )
            speed = sampled[0:8]
            for b in range(1, CHUNK // 64):
                speed = jnp.where(lane8 // 64 == b, sampled[8 * b : 8 * b + 8], speed)
            for b, home in enumerate(homes):
                for j in range(4):
                    force[j, pl.ds(home, 8), :] += spread[
                        8 * b : 8 * b + 8, 128 * j : 128 * j + 128
                    ]
            before = jnp.where(
                third == 0,
                jnp.broadcast_to(bead[6:7, :], (8, CHUNK)),
                jnp.where(
                    third == 1,
                    jnp.broadcast_to(bead[7:8, :], (8, CHUNK)),
                    jnp.broadcast_to(last[pl.ds(slot, 1), at], (8, CHUNK)),
                ),
            )
            vertex_out[0, 0, slot, 0:8, at] = jnp.where(
                row8 < 6, bead + 0.5 * (before + speed), speed
            )
            vertex_out[0, 0, slot, 8:9, at] = speed[2:3, :]
        return carry

    lax.fori_loop(0, count, couple, 0)

    for k in range(3):
        for bz in range(2):
            for j in range(4):
                base = bz * 2 * 16 * 8 + 3 + k
                zero = force[j, pl.ds(base, 16, stride=8), :]
                one = force[j, pl.ds(base + 128, 16, stride=8), :]
                turn[pl.ds(2 * j, 16, stride=8), :] = jnp.where(left, zero, pltpu.roll(one, 64, 1))
                turn[pl.ds(2 * j + 1, 16, stride=8), :] = jnp.where(
                    left, pltpu.roll(zero, 64, 1), one
                )
            back = turn[...].T
            for bx in range(2):
                for iz in range(8):
                    first = (8 * bz + iz) * CX + 8 * bx
                    flow[4 + k, first : first + 8, :] = back[(bx * 8 + iz) * 8 : (bx * 8 + iz) * 8 + 8]

    def collide(z, carry):
        at = pl.ds(pl.multiple_of(z * CX, CX), CX)
        density = flow[0, at, :]
        inverse = 1.0 / density
        body = [flow[4 + k, at, :] for k in range(3)]
        speed = [(flow[1 + k, at, :] + 0.5 * body[k]) * inverse for k in range(3)]
        square = speed[0] * speed[0] + speed[1] * speed[1] + speed[2] * speed[2]
        work = speed[0] * body[0] + speed[1] * body[1] + speed[2] * body[2]
        common = density * (1.25 - 1.875 * square) - 1.125 * work
        wall = solid[at, :] == 1
        read[0, at, :] = jnp.where(wall, read[0, at, :], WEIGHTS[0] * common - 0.25 * read[0, at, :])
        steep = 5.625 * density
        slope = 3.75 * density
        for q in range(1, 19, 2):
            along, push_along = None, None
            for c, s, b in zip(LATTICE[q], speed, body):
                if c != 0:
                    s, b = (s, b) if c > 0 else (-s, -b)
                    along = s if along is None else along + s
                    push_along = b if push_along is None else push_along + b
            even = WEIGHTS[q] * (common + along * (steep * along + 3.375 * push_along))
            odd = WEIGHTS[q] * (slope * along + 1.125 * push_along)
            here, there = read[q, at, :], read[q + 1, at, :]
            read[q, at, :] = jnp.where(wall, there, even + odd - 0.25 * here)
            read[q + 1, at, :] = jnp.where(wall, here, even - odd - 0.25 * there)
        return carry

    def ship(part):
        span = slice(part * 64, (part + 1) * 64)
        return pltpu.make_async_copy(
            read.at[:, span, :], pops_out.at[:, span, :], out_sem.at[part]
        )

    for part in range(4):
        lax.fori_loop(part * 4, part * 4 + 4, collide, 0)
        ship(part).start()
    for part in range(4):
        ship(part).wait()


def step(leave, bricks, pops, solid, states, faces, corners, stiffness):
    vmem = pl.BlockSpec(memory_space=pltpu.VMEM)
    smem = pl.BlockSpec(memory_space=pltpu.SMEM)
    hbm = pl.BlockSpec(memory_space=pl.ANY)
    return pl.pallas_call(
        step_kernel,
        out_shape=[
            jax.ShapeDtypeStruct((19, NZ * CX, CY), F32),
            jax.ShapeDtypeStruct((1, 1, ALL, 9, VERT), F32),
        ],
        in_specs=[smem, smem] + [vmem] * 12,
        out_specs=[hbm, vmem],
        scratch_shapes=[
            pltpu.VMEM((19, NZ * CX, CY), F32),
            pltpu.VMEM((7, NZ * CX, CY), F32),
            pltpu.VMEM((10, NZ, CY), F32),
            pltpu.VMEM((10, CX, CY), F32),
            pltpu.VMEM((128, 128), F32),
            pltpu.VMEM((4, 512, 128), F32),
            pltpu.VMEM((4, 512, 128), F32),
            pltpu.VMEM((ALL, 8, VERT), F32),
            pltpu.VMEM((ALL, VERT), F32),
            pltpu.VMEM((ALL * 8, VERT), F32),
            pltpu.VMEM((2, 512, CHUNK), BF16),
            pltpu.SMEM((4, 8, 128), F32),
            pltpu.SMEM((ALL + 1,), jnp.int32),
            pltpu.SemaphoreType.DMA((4,)),
            pltpu.SemaphoreType.DMA((4,)),
        ],
        compiler_params=pltpu.CompilerParams(vmem_limit_bytes=48 << 20),
        name="lattice_step",
    )(leave, bricks, pops, solid, states, *faces, *corners, stiffness)


def along_axis(x, axis, by):
    size = lax.axis_size(axis)
    return lax.ppermute(x, axis, [(i, (i + by) % size) for i in range(size)])


def across(x, dx, dy):
    nx, ny = lax.axis_size("gx"), lax.axis_size("gy")
    pairs = [
        (a * ny + b, (a + dx) % nx * ny + (b + dy) % ny) for a in range(nx) for b in range(ny)
    ]
    return lax.ppermute(x, ("gx", "gy"), pairs)


def local(populations, solid_mask, bead_states, bead_bricks, leave_dir, stiffness):
    pops = populations.reshape(19, NZ * CX, CY)
    solid = solid_mask.reshape(NZ * CX, CY)
    packed = pack(leave_dir, bead_bricks, pops, bead_states)
    faces = [
        along_axis(packed[0], "gx", 1),
        along_axis(packed[1], "gx", -1),
        along_axis(packed[2], "gy", 1),
        along_axis(packed[3], "gy", -1),
    ]
    corners = [across(x, dx, dy) for x, (_, dx, dy) in zip(packed[4:], CORNERS)]
    pops_out, vertex_out = step(
        leave_dir, bead_bricks, pops, solid, bead_states, faces, corners, stiffness
    )
    return (pops_out.reshape(populations.shape), vertex_out)


def solution(mesh):
    return jax.shard_map(
        local,
        mesh=mesh,
        in_specs=(
            P(None, None, "gx", "gy"),
            P(None, "gx", "gy"),
            P("gx", "gy", None, None, None),
            P("gx", "gy", None, None),
            P("gx", "gy", None),
            P(),
        ),
        out_specs=(P(None, None, "gx", "gy"), P("gx", "gy", None, None, None)),
        check_vma=False,
    )
```

profile of v0, /device:TPU:71, one launch (start us, length us, event | category | flops | bytes accessed | tf_op | source)
XLA Modules:
  0.0 63.0 jit_solution(855666262032489605)
XLA Ops:
  0.6 0.0 copy-start.6
  0.6 0.0 copy-start.4
  0.7 0.0 copy-start.2
  0.7 1.2 %copy.9.states = f32[1,1,8,9,1280]{4,3,2,1,0:T(8,128)S(1)} copy(f32[1,1,8,9,1280]{4,2,3,1,0:T(8,128)} %param.8) | data formatting | bytes 737280 | tf_op args[2]
  1.8 0.0 copy-start
  1.8 1.7 %copy-done = f32[19,16,16,128]{3,2,1,0:T(8,128)S(1)} copy-done((f32[19,16,16,128]{3,2,1,0:T(8,128)S(1)}, f32[19,16,16,128]{3,2,1,0:T(8,128)}, u32[]{:S(2)}) %copy-start) | copy-done | bytes 2490392
  3.5 0.0 copy-start.3
  3.5 0.7 %copy-done.3 = s32[1,1,8,20]{3,2,1,0:T(8,128)S(1)} copy-done((s32[1,1,8,20]{3,2,1,0:T(8,128)S(1)}, s32[1,1,8,20]{3,2,1,0:T(8,128)}, u32[]{:S(2)}) %copy-start.3) | copy-done | bytes 664
  4.2 0.0 copy-start.5
  4.2 0.7 %copy-done.5 = s32[1,1,8]{2,1,0:T(1,128)S(1)} copy-done((s32[1,1,8]{2,1,0:T(1,128)S(1)}, s32[1,1,8]{2,1,0:T(1,128)}, u32[]{:S(2)}) %copy-start.5) | copy-done | bytes 56
  4.9 0.0 copy-start.1
  4.9 1.0 %pack_messages.1 = (f32[32,1280]{1,0:T(8,128)S(1)}, f32[32,1280]{1,0:T(8,128)S(1)}, f32[32,1280]{1,0:T(8,128)S(1)}, f32[32,1280]{1,0:T(8,128)S(1)}, f32[8,128]{1...) custom-call(s32[1,1,8]{2,1,0:T(1,128)S(1)} %copy-done.5, ...), custom_call_target="tpu_custom_call" | custom-call | tf_op jit(solution)/shard_map/pack_messages/pallas_call | solution.py:94
  5.9 4.8 %collective-permute-start = (f32[32,1280]{1,0:T(8,128)S(1)}, f32[32,1280]{1,0:T(8,128)S(1)}, u32[]{:S(2)}, u32[]{:S(2)}) collective-permute-start(f32[32,1280]{1,0:T(8,128)S(1)} %get-tuple-element.12), channel_id=1, source_target_pairs={{0,8},{8,16},{16,24},{24,32},{32,40},{40,48},{48,56},{56,64},{64,7... | collective-permute-start | bytes 491528 | tf_op jit(solution)/shard_map/ppermute | solution.py:419
  10.6 0.0 collective-permute-start.1
  10.6 0.7 %collective-permute-start.2 = (f32[32,1280]{1,0:T(8,128)S(1)}, f32[32,1280]{1,0:T(8,128)S(1)}, u32[]{:S(2)}, u32[]{:S(2)}) collective-permute-start(f32[32,1280]{1,0:T(8,128)S(1)} %get-tuple-element.14), channel_id=1, source_target_pairs={{0,1},{1,2},{2,3},{3,4},{4,5},{5,6},{6,7},{7,0},{8,9},{9,10},{10,1... | collective-permute-start | bytes 491528 | tf_op jit(solution)/shard_map/ppermute | solution.py:419
  11.4 2.8 %collective-permute-start.3 = (f32[32,1280]{1,0:T(8,128)S(1)}, f32[32,1280]{1,0:T(8,128)S(1)}, u32[]{:S(2)}, u32[]{:S(2)}) collective-permute-start(f32[32,1280]{1,0:T(8,128)S(1)} %get-tuple-element.15), channel_id=1, source_target_pairs={{0,7},{1,0},{2,1},{3,2},{4,3},{5,4},{6,5},{7,6},{8,15},{9,8},{10,9... | collective-permute-start | bytes 491528 | tf_op jit(solution)/shard_map/ppermute | solution.py:419
  14.2 4.9 %collective-permute-start.4 = (f32[8,128]{1,0:T(8,128)S(1)}, f32[8,128]{1,0:T(8,128)S(1)}, u32[]{:S(2)}, u32[]{:S(2)}) collective-permute-start(f32[8,128]{1,0:T(8,128)S(1)} %get-tuple-element.16), channel_id=1, source_target_pairs={{0,9},{1,10},{2,11},{3,12},{4,13},{5,14},{6,15},{7,8},{8,17},{9,18... | collective-permute-start | bytes 12296 | tf_op jit(solution)/shard_map/ppermute | solution.py:427
  19.1 2.1 %collective-permute-done.4.c_pp = f32[8,128]{1,0:T(8,128)S(1)} collective-permute-done((f32[8,128]{1,0:T(8,128)S(1)}, f32[8,128]{1,0:T(8,128)S(1)}, u32[]{:S(2)}, u32[]{:S(2)}) %collective-permute-start.4) | collective-permute-done | bytes 4128 | tf_op jit(solution)/shard_map/ppermute | solution.py:427
  21.2 0.0 collective-permute-start.5
  21.2 8.9 %collective-permute-done.5.c_mm = f32[8,128]{1,0:T(8,128)S(1)} collective-permute-done((f32[8,128]{1,0:T(8,128)S(1)}, f32[8,128]{1,0:T(8,128)S(1)}, u32[]{:S(2)}, u32[]{:S(2)}) %collective-permute-start.5) | collective-permute-done | bytes 4128 | tf_op jit(solution)/shard_map/ppermute | solution.py:427
  30.0 6.3 %collective-permute-start.6 = (f32[8,128]{1,0:T(8,128)S(1)}, f32[8,128]{1,0:T(8,128)S(1)}, u32[]{:S(2)}, u32[]{:S(2)}) collective-permute-start(f32[8,128]{1,0:T(8,128)S(1)} %get-tuple-element.18), channel_id=1, source_target_pairs={{0,15},{1,8},{2,9},{3,10},{4,11},{5,12},{6,13},{7,14},{8,23},{9,16... | collective-permute-start | bytes 12296 | tf_op jit(solution)/shard_map/ppermute | solution.py:427
  36.4 0.8 %collective-permute-done.6.c_pm = f32[8,128]{1,0:T(8,128)S(1)} collective-permute-done((f32[8,128]{1,0:T(8,128)S(1)}, f32[8,128]{1,0:T(8,128)S(1)}, u32[]{:S(2)}, u32[]{:S(2)}) %collective-permute-start.6) | collective-permute-done | bytes 4128 | tf_op jit(solution)/shard_map/ppermute | solution.py:427
  37.1 0.0 collective-permute-start.7
  37.2 10.8 %collective-permute-done.7.c_mp = f32[8,128]{1,0:T(8,128)S(1)} collective-permute-done((f32[8,128]{1,0:T(8,128)S(1)}, f32[8,128]{1,0:T(8,128)S(1)}, u32[]{:S(2)}, u32[]{:S(2)}) %collective-permute-start.7) | collective-permute-done | bytes 4128 | tf_op jit(solution)/shard_map/ppermute | solution.py:427
  47.9 0.0 collective-permute-done.x_low
  47.9 0.0 collective-permute-done.1.x_high
  48.0 0.0 collective-permute-done.2.y_low
  48.0 0.0 collective-permute-done.3.y_high
  48.0 0.0 copy-done.6
  48.0 0.0 copy-done.4
  48.0 0.0 copy-done.2
  48.0 0.0 copy-done.1
  48.0 13.7 %lattice_step.1 = (f32[19,256,128]{2,1,0:T(8,128)}, f32[1,1,16,9,1280]{4,3,2,1,0:T(8,128)S(1)}) custom-call(s32[1,1,8]{2,1,0:T(1,128)S(1)} %copy-done.6, s32[1,1,8,20]{3,2,1,0:T(8,128)S(1)} %copy-done.4, f32[19,256,128]{2,1,0:T(8,128)S(1)} %bitcast.4, s32[256,128]{1,0:T(8,128)S(1)} %bitcast.5, f32[1,1,8,9,1280]{4,3,2,1,0:T(8,128)S(1)} %copy.9.states, ...), custom_call_target="tpu_custom_call" | custom-call | tf_op jit(solution)/shard_map/lattice_step/pallas_call | solution.py:387
  61.7 1.3 %copy.10 = f32[1,1,16,9,1280]{4,2,3,1,0:T(8,128)} copy(f32[1,1,16,9,1280]{4,3,2,1,0:T(8,128)S(1)} %get-tuple-element.23) | data formatting | bytes 1474560
Async XLA Ops:
  0.6 47.3 %copy-start.6 = (s32[1,1,8]{2,1,0:T(1,128)S(1)}, s32[1,1,8]{2,1,0:T(1,128)}, u32[]{:S(2)}) copy-start(s32[1,1,8]{2,1,0:T(1,128)} %leave.3) | copy-start | bytes 100
  0.6 47.3 %copy-start.4 = (s32[1,1,8,20]{3,2,1,0:T(8,128)S(1)}, s32[1,1,8,20]{3,2,1,0:T(8,128)}, u32[]{:S(2)}) copy-start(s32[1,1,8,20]{3,2,1,0:T(8,128)} %bricks.3) | copy-start | bytes 1924
  0.7 47.3 %copy-start.2 = (s32[16,16,128]{2,1,0:T(8,128)S(1)}, s32[16,16,128]{2,1,0:T(8,128)}, u32[]{:S(2)}) copy-start(s32[16,16,128]{2,1,0:T(8,128)} %param.7) | copy-start | bytes 393220
  1.8 1.7 %copy-start = (f32[19,16,16,128]{3,2,1,0:T(8,128)S(1)}, f32[19,16,16,128]{3,2,1,0:T(8,128)}, u32[]{:S(2)}) copy-start(f32[19,16,16,128]{3,2,1,0:T(8,128)} %param.6) | copy-start | bytes 7471108
  3.5 0.7 %copy-start.3 = (s32[1,1,8,20]{3,2,1,0:T(8,128)S(1)}, s32[1,1,8,20]{3,2,1,0:T(8,128)}, u32[]{:S(2)}) copy-start(s32[1,1,8,20]{3,2,1,0:T(8,128)} %bricks.3) | copy-start | bytes 1924
  4.2 0.7 %copy-start.5 = (s32[1,1,8]{2,1,0:T(1,128)S(1)}, s32[1,1,8]{2,1,0:T(1,128)}, u32[]{:S(2)}) copy-start(s32[1,1,8]{2,1,0:T(1,128)} %leave.3) | copy-start | bytes 100
  4.9 43.1 %copy-start.1 = (f32[19,16,16,128]{3,2,1,0:T(8,128)S(1)}, f32[19,16,16,128]{3,2,1,0:T(8,128)}, u32[]{:S(2)}) copy-start(f32[19,16,16,128]{3,2,1,0:T(8,128)} %param.6) | copy-start | bytes 7471108
  5.9 42.1 %collective-permute-start = (f32[32,1280]{1,0:T(8,128)S(1)}, f32[32,1280]{1,0:T(8,128)S(1)}, u32[]{:S(2)}, u32[]{:S(2)}) collective-permute-start(f32[32,1280]{1,0:T(8,128)S(1)} %get-tuple-element.12), channel_id=1, source_target_pairs={{0,8},{8,16},{16,24},{24,32},{32,40},{40,48},{48,56},{56,64},{64,7... | collective-permute-start | bytes 491528 | tf_op jit(solution)/shard_map/ppermute | solution.py:419
  10.6 37.3 %collective-permute-start.1 = (f32[32,1280]{1,0:T(8,128)S(1)}, f32[32,1280]{1,0:T(8,128)S(1)}, u32[]{:S(2)}, u32[]{:S(2)}) collective-permute-start(f32[32,1280]{1,0:T(8,128)S(1)} %get-tuple-element.13), channel_id=1, source_target_pairs={{0,248},{8,0},{16,8},{24,16},{32,24},{40,32},{48,40},{56,48},{64,5... | collective-permute-start | bytes 491528 | tf_op jit(solution)/shard_map/ppermute | solution.py:419
  10.6 37.3 %collective-permute-start.2 = (f32[32,1280]{1,0:T(8,128)S(1)}, f32[32,1280]{1,0:T(8,128)S(1)}, u32[]{:S(2)}, u32[]{:S(2)}) collective-permute-start(f32[32,1280]{1,0:T(8,128)S(1)} %get-tuple-element.14), channel_id=1, source_target_pairs={{0,1},{1,2},{2,3},{3,4},{4,5},{5,6},{6,7},{7,0},{8,9},{9,10},{10,1... | collective-permute-start | bytes 491528 | tf_op jit(solution)/shard_map/ppermute | solution.py:419
  11.4 36.6 %collective-permute-start.3 = (f32[32,1280]{1,0:T(8,128)S(1)}, f32[32,1280]{1,0:T(8,128)S(1)}, u32[]{:S(2)}, u32[]{:S(2)}) collective-permute-start(f32[32,1280]{1,0:T(8,128)S(1)} %get-tuple-element.15), channel_id=1, source_target_pairs={{0,7},{1,0},{2,1},{3,2},{4,3},{5,4},{6,5},{7,6},{8,15},{9,8},{10,9... | collective-permute-start | bytes 491528 | tf_op jit(solution)/shard_map/ppermute | solution.py:419
  14.2 7.0 %collective-permute-start.4 = (f32[8,128]{1,0:T(8,128)S(1)}, f32[8,128]{1,0:T(8,128)S(1)}, u32[]{:S(2)}, u32[]{:S(2)}) collective-permute-start(f32[8,128]{1,0:T(8,128)S(1)} %get-tuple-element.16), channel_id=1, source_target_pairs={{0,9},{1,10},{2,11},{3,12},{4,13},{5,14},{6,15},{7,8},{8,17},{9,18... | collective-permute-start | bytes 12296 | tf_op jit(solution)/shard_map/ppermute | solution.py:427
  21.2 8.9 %collective-permute-start.5 = (f32[8,128]{1,0:T(8,128)S(1)}, f32[8,128]{1,0:T(8,128)S(1)}, u32[]{:S(2)}, u32[]{:S(2)}) collective-permute-start(f32[8,128]{1,0:T(8,128)S(1)} %get-tuple-element.17), channel_id=1, source_target_pairs={{0,255},{1,248},{2,249},{3,250},{4,251},{5,252},{6,253},{7,254},{8... | collective-permute-start | bytes 12296 | tf_op jit(solution)/shard_map/ppermute | solution.py:427
  30.0 7.1 %collective-permute-start.6 = (f32[8,128]{1,0:T(8,128)S(1)}, f32[8,128]{1,0:T(8,128)S(1)}, u32[]{:S(2)}, u32[]{:S(2)}) collective-permute-start(f32[8,128]{1,0:T(8,128)S(1)} %get-tuple-element.18), channel_id=1, source_target_pairs={{0,15},{1,8},{2,9},{3,10},{4,11},{5,12},{6,13},{7,14},{8,23},{9,16... | collective-permute-start | bytes 12296 | tf_op jit(solution)/shard_map/ppermute | solution.py:427
  37.1 10.8 %collective-permute-start.7 = (f32[8,128]{1,0:T(8,128)S(1)}, f32[8,128]{1,0:T(8,128)S(1)}, u32[]{:S(2)}, u32[]{:S(2)}) collective-permute-start(f32[8,128]{1,0:T(8,128)S(1)} %get-tuple-element.19), channel_id=1, source_target_pairs={{0,249},{1,250},{2,251},{3,252},{4,253},{5,254},{6,255},{7,248},{8... | collective-permute-start | bytes 12296 | tf_op jit(solution)/shard_map/ppermute | solution.py:427
where the time goes:
time: 63.2 us; the launch traced here: 63 us
  waiting for transfers between devices  22.5 us (36%)
  starting transfers between devices  19.6 us (31%)
  Pallas kernels  14.7 us (23%)
  local copies, waits for them, and re-layouts  5.52 us (9%)
  between operations  0.73 us (1%)
    ppermute x4, waiting for transfers between devices, across(): return lax.ppermute(x, ('gx', 'gy'), pairs)  22.5 us
    pallas_call x1, Pallas kernels, step(): pl.pallas_call(step_kernel, out_shape=[jax.ShapeDtypeStruct((19, NZ * CX,...  13.7 us
    ppermute x4, starting transfers between devices, across(): return lax.ppermute(x, ('gx', 'gy'), pairs)  11.2 us
    ppermute x4, starting transfers between devices, along_axis(): return lax.ppermute(x, axis, [(i, (i + by) % size) for i in range(size)])  8.33 us
    unnamed x16, local copies, waits for them, and re-layouts  5.52 us
  transfers between devices with their start and end apart: 8, of which 4 were waited for; matrix products, arithmetic and copies ran while one was open for 0% of the time, Pallas kernels for 0%

commit v1 on v0

v1 whole, which is shorter than its diff:
```python
import functools

import jax
import jax.numpy as jnp
import numpy as np
from jax import lax
from jax.experimental import pallas as pl
from jax.experimental.pallas import tpu as pltpu
from jax.sharding import PartitionSpec as P

LATTICE = [
    (0, 0, 0),
    (1, 0, 0),
    (-1, 0, 0),
    (0, 1, 0),
    (0, -1, 0),
    (0, 0, 1),
    (0, 0, -1),
    (1, 1, 0),
    (-1, -1, 0),
    (1, -1, 0),
    (-1, 1, 0),
    (1, 0, 1),
    (-1, 0, -1),
    (1, 0, -1),
    (-1, 0, 1),
    (0, 1, 1),
    (0, -1, -1),
    (0, 1, -1),
    (0, -1, 1),
]
WEIGHTS = [1.0 / 3.0] + [1.0 / 18.0] * 6 + [1.0 / 36.0] * 12
X_UP = [1, 7, 9, 11, 13]
X_DOWN = [2, 8, 10, 12, 14]
Y_UP = [3, 7, 10, 15, 17]
Y_DOWN = [4, 8, 9, 16, 18]
NZ, CX, CY = 16, 16, 128
SLOTS, SIDES, MIG, ALL = 8, 4, 2, 16
VERT, BLOCKS, CHUNK = 1280, 20, 256
F32, BF16 = jnp.float32, jnp.bfloat16


def lanes(shape):
    return lax.broadcasted_iota(jnp.int32, shape, len(shape) - 1)


def rows(shape):
    return lax.broadcasted_iota(jnp.int32, shape, len(shape) - 2)


BEAD_ROWS, FLAG_ROWS, FACE_ROWS = 180, 180, 184
X_ROWS, Y_ROWS = FACE_ROWS + 5 * NZ, FACE_ROWS + CX


def pick(leave, code):
    first, second, count = jnp.int32(0), jnp.int32(0), jnp.int32(0)
    for slot in range(SLOTS):
        hit = leave[0, 0, slot] == code
        first = jnp.where(hit & (count == 0), slot, first)
        second = jnp.where(hit & (count == 1), slot, second)
        count = count + hit.astype(jnp.int32)
    return (first, second), count


def pack_beads(out, code, leave, bricks, states):
    chosen, count = pick(leave, code)
    out[176:184, :] = jnp.zeros((8, 128), F32)
    for place, slot in enumerate(chosen):
        for entry in range(9):
            row = states[entry, pl.ds(slot, 1), :]
            for c in range(VERT // 128):
                at = 18 * c + 2 * entry + place
                out[at : at + 1, :] = row[:, 128 * c : 128 * c + 128]
        valid = (count > place).astype(F32)
        at = FLAG_ROWS + place
        out[at : at + 1, :] = jnp.full((1, 128), 1.0, F32) * valid
        out[at : at + 1, 0:BLOCKS] = bricks[pl.ds(slot, 1), :].astype(F32)


def fetch_beads(leave_hbm, bricks_hbm, states_hbm, leave, bricks, states, sem):
    return [
        pltpu.make_async_copy(leave_hbm, leave, sem.at[0]),
        pltpu.make_async_copy(bricks_hbm.at[0, 0], bricks, sem.at[1]),
        pltpu.make_async_copy(states_hbm.at[0, 0], states, sem.at[2]),
    ]


def pack_x_kernel(
    leave_hbm, bricks_hbm, states_hbm, pops_hbm, up, down, leave, bricks, states, sem, face_sem
):
    copies = fetch_beads(leave_hbm, bricks_hbm, states_hbm, leave, bricks, states, sem)
    for side, (out, group, x) in enumerate(((up, X_UP, CX - 1), (down, X_DOWN, 0))):
        for i, q in enumerate(group):
            at = FACE_ROWS + NZ * i
            copies.append(
                pltpu.make_async_copy(
                    pops_hbm.at[q, :, x, :], out.at[at : at + NZ, :], face_sem.at[side * 5 + i]
                )
            )
    for copy in copies:
        copy.start()
    for copy in copies[:3]:
        copy.wait()
    pack_beads(up, 1, leave, bricks, states)
    pack_beads(down, 2, leave, bricks, states)
    for copy in copies[3:]:
        copy.wait()


Y_RANGES = ((3, 5), (7, 11), (15, 19))
Y_PLACE = {q: n for n, q in enumerate(q for lo, hi in Y_RANGES for q in range(lo, hi))}


def pack_y_kernel(
    leave_hbm, bricks_hbm, states_hbm, pops_hbm, up, down,
    leave, bricks, states, pops, sem, pops_sem,
):
    copies = fetch_beads(leave_hbm, bricks_hbm, states_hbm, leave, bricks, states, sem)
    for n, (lo, hi) in enumerate(Y_RANGES):
        at = Y_PLACE[lo]
        copies.append(
            pltpu.make_async_copy(
                pops_hbm.at[lo:hi], pops.at[at : at + hi - lo], pops_sem.at[n]
            )
        )
    for copy in copies:
        copy.start()
    for copy in copies[:3]:
        copy.wait()
    pack_beads(up, 3, leave, bricks, states)
    pack_beads(down, 4, leave, bricks, states)
    for copy in copies[3:]:
        copy.wait()
    lane = lanes((CX, CY))
    for out, group, y in ((up, Y_UP, CY - 1), (down, Y_DOWN, 0)):
        column = jnp.zeros((CX, CY), F32)
        for i, q in enumerate(group):
            for z in range(NZ):
                place = i * NZ + z
                column = jnp.where(
                    lane == place, pltpu.roll(pops[Y_PLACE[q], z], (place - y) % CY, 1), column
                )
        out[FACE_ROWS : FACE_ROWS + CX, :] = column


EDGES_UP = ((7, 0), (10, 1))
EDGES_DOWN = ((9, 0), (8, 1))


def edge_kernel(up, down, x_low, x_high, up_out, down_out):
    lane = lanes((NZ, CY))
    for source, out, edges, y in ((up, up_out, EDGES_UP, CY - 1), (down, down_out, EDGES_DOWN, 0)):
        out[0:FACE_ROWS, :] = source[0:FACE_ROWS, :]
        column = source[FACE_ROWS : FACE_ROWS + CX, :]
        for n, (q, side) in enumerate(edges):
            group, message = ((X_UP, x_low), (X_DOWN, x_high))[side]
            at = FACE_ROWS + NZ * group.index(q)
            moved = pltpu.roll(message[at : at + NZ, :], (80 + n - y) % CY, 1)
            column = jnp.where(lane == 80 + n, moved, column)
        out[FACE_ROWS : FACE_ROWS + CX, :] = column


VMEM = pl.BlockSpec(memory_space=pltpu.VMEM)
HBM = pl.BlockSpec(memory_space=pltpu.HBM)
BEAD_SCRATCH = [
    pltpu.SMEM((1, 1, SLOTS), jnp.int32),
    pltpu.VMEM((SLOTS, BLOCKS), jnp.int32),
    pltpu.VMEM((9, SLOTS, VERT), F32),
]


def pack_x(leave, bricks, states, pops):
    return pl.pallas_call(
        pack_x_kernel,
        out_shape=[jax.ShapeDtypeStruct((X_ROWS, 128), F32)] * 2,
        in_specs=[HBM] * 4,
        out_specs=[VMEM] * 2,
        scratch_shapes=BEAD_SCRATCH
        + [pltpu.SemaphoreType.DMA((3,)), pltpu.SemaphoreType.DMA((10,))],
        compiler_params=pltpu.CompilerParams(vmem_limit_bytes=60 << 20),
        cost_estimate=pl.CostEstimate(flops=10**6, bytes_accessed=10**6, transcendentals=0),
        name="pack_x",
    )(leave, bricks, states, pops)


def pack_y(leave, bricks, states, pops):
    return pl.pallas_call(
        pack_y_kernel,
        out_shape=[jax.ShapeDtypeStruct((Y_ROWS, 128), F32)] * 2,
        in_specs=[HBM] * 4,
        out_specs=[VMEM] * 2,
        scratch_shapes=BEAD_SCRATCH
        + [
            pltpu.VMEM((10, NZ, CX, CY), F32),
            pltpu.SemaphoreType.DMA((3,)),
            pltpu.SemaphoreType.DMA((3,)),
        ],
        compiler_params=pltpu.CompilerParams(vmem_limit_bytes=8 << 20),
        cost_estimate=pl.CostEstimate(flops=10**6, bytes_accessed=2 * 10**6, transcendentals=0),
        name="pack_y",
    )(leave, bricks, states, pops)


def add_edges(up, down, x_low, x_high):
    return pl.pallas_call(
        edge_kernel,
        out_shape=[jax.ShapeDtypeStruct((Y_ROWS, 128), F32)] * 2,
        in_specs=[VMEM] * 4,
        out_specs=[VMEM] * 2,
        compiler_params=pltpu.CompilerParams(vmem_limit_bytes=8 << 20),
        name="add_edges",
    )(up, down, x_low, x_high)


def phi(distance):
    t = distance * distance
    value = jnp.full(t.shape, COSINE[-1], F32)
    for coefficient in COSINE[-2::-1]:
        value = value * t + coefficient
    return jnp.where(jnp.abs(distance) < 2.0, 0.5 * (value * value), 0.0)


def cosine_terms():
    terms, term = [], 1.0
    for n in range(8):
        terms.append(float(term))
        term = -term * (np.pi / 4) ** 2 / ((2 * n + 1) * (2 * n + 2))
    return terms


COSINE = cosine_terms()
PER_CHUNK = CHUNK // 64


def fill_table(table, states, slot, at):
    step8 = rows((8, CHUNK)).astype(F32)
    along_x, along_y, along_z = [
        phi(jnp.broadcast_to(states[k, pl.ds(slot, 1), at], (8, CHUNK)) - step8) for k in range(3)
    ]
    planes = [jnp.broadcast_to(along_z[iz : iz + 1, :], (8, CHUNK)) * along_x for iz in range(8)]
    for iy in range(8):
        factor = jnp.broadcast_to(along_y[iy : iy + 1, :], (8, CHUNK))
        for pair in range(4):
            both = jnp.concatenate(
                [planes[2 * pair] * factor, planes[2 * pair + 1] * factor], axis=0
            )
            first = iy * 64 + pair * 16
            table[first : first + 16, :] = both.astype(BF16)


def stiff_product(push, states, stiffness):
    shape = states[3:6].reshape(24, VERT).astype(BF16)
    for n in range(5):
        at = slice(n * 256, (n + 1) * 256)
        push[:, at] = -jnp.dot(shape, stiffness[:, at], preferred_element_type=F32)


def spread_chunk(force, table, push, slot, at, homes):
    row8 = rows((8, CHUNK))
    block = lanes((8, CHUNK)) // 64
    parts = [
        jnp.broadcast_to(push[pl.ds(8 * k + slot, 1), at], (8, CHUNK)) for k in range(3)
    ]
    drive = jnp.where(row8 == 0, parts[0], jnp.where(row8 == 1, parts[1], parts[2]))
    drives = jnp.concatenate(
        [jnp.where(block == b, drive, 0.0) for b in range(PER_CHUNK)], axis=0
    ).astype(BF16)
    spread = lax.dot_general(
        drives, table[...], (((1,), (1,)), ((), ())), preferred_element_type=F32
    )
    for b, home in enumerate(homes):
        for j in range(4):
            force[j, pl.ds(home, 8), :] += spread[8 * b : 8 * b + 8, 128 * j : 128 * j + 128]


def sample_chunk(sampled_speed, cells, table, slot, at, homes):
    block = lanes((8, CHUNK)) // 64
    nearby = jnp.concatenate(
        [
            jnp.concatenate([cells[j, pl.ds(home, 8), :] for j in range(4)], axis=1)
            for home in homes
        ],
        axis=0,
    ).astype(BF16)
    sampled = jnp.dot(nearby, table[...], preferred_element_type=F32)
    speed = sampled[0:8]
    for b in range(1, PER_CHUNK):
        speed = jnp.where(block == b, sampled[8 * b : 8 * b + 8], speed)
    for k in range(3):
        sampled_speed[k, pl.ds(slot, 1), at] = speed[k : k + 1, :]


def list_active(order, flags):
    count = jnp.int32(0)
    for slot, flag in enumerate(flags):
        order[count] = slot
        count = count + flag.astype(jnp.int32)
    return count


def own_kernel(
    leave_hbm, bricks_hbm, states, stiffness, force, leave, bricks, push, tables, order, sem
):
    copies = [
        pltpu.make_async_copy(leave_hbm, leave, sem.at[0]),
        pltpu.make_async_copy(bricks_hbm, bricks, sem.at[1]),
    ]
    for copy in copies:
        copy.start()
    stiff_product(push, states.at[0, 0], stiffness)
    force[...] = jnp.zeros(force.shape, F32)
    for copy in copies:
        copy.wait()
    count = list_active(order, [leave[0, 0, slot] == 0 for slot in range(SLOTS)])

    def couple(turn_number, carry):
        slot = order[turn_number]
        for chunk in range(VERT // CHUNK):
            at = slice(chunk * CHUNK, (chunk + 1) * CHUNK)
            table = tables.at[chunk % 2]
            fill_table(table, states.at[0, 0], slot, at)
            homes = [
                pl.multiple_of(bricks[0, 0, slot, chunk * PER_CHUNK + b] * 8, 8)
                for b in range(PER_CHUNK)
            ]
            spread_chunk(force, table, push, slot, at, homes)
        return carry

    lax.fori_loop(0, count, couple, 0)


def spread_own(leave, bricks, states, stiffness):
    return pl.pallas_call(
        own_kernel,
        out_shape=jax.ShapeDtypeStruct((4, 512, 128), F32),
        in_specs=[HBM, HBM, VMEM, VMEM],
        out_specs=VMEM,
        scratch_shapes=[
            pltpu.SMEM((1, 1, SLOTS), jnp.int32),
            pltpu.SMEM((1, 1, SLOTS, BLOCKS), jnp.int32),
            pltpu.VMEM((24, VERT), F32),
            pltpu.VMEM((2, 512, CHUNK), BF16),
            pltpu.SMEM((SLOTS + 1,), jnp.int32),
            pltpu.SemaphoreType.DMA((2,)),
        ],
        compiler_params=pltpu.CompilerParams(vmem_limit_bytes=16 << 20),
        cost_estimate=pl.CostEstimate(
            flops=2 * 10**9, bytes_accessed=5 * 10**6, transcendentals=0
        ),
        name="spread_own",
    )(leave, bricks, states, stiffness)


def step_kernel(
    leave_hbm, bricks_hbm, pops, solid, states_in, own_force,
    x_low, x_high, y_low, y_high,
    stiffness,
    pops_out, vertex_out,
    read, flow, halo_y, turn, cells, force, guests, push, tables, speeds, vertex,
    leave, bricks, meta, order, meta_sem, out_sem,
):
    faces = (x_low, x_high, y_low, y_high)
    states = states_in.at[0, 0]
    copies = [
        pltpu.make_async_copy(faces[side].at[176:184, :], meta.at[side], meta_sem.at[side])
        for side in range(4)
    ] + [
        pltpu.make_async_copy(leave_hbm, leave, meta_sem.at[4]),
        pltpu.make_async_copy(bricks_hbm, bricks, meta_sem.at[5]),
    ]
    for copy in copies:
        copy.start()

    for side in range(4):
        for c in range(VERT // 128):
            for entry in range(9):
                guests[entry, 2 * side : 2 * side + 2, 128 * c : 128 * c + 128] = faces[side][
                    18 * c + 2 * entry : 18 * c + 2 * entry + 2, :
                ]

    row16 = rows((CX, CY))
    lane16 = lanes((CX, CY))
    for side, group in enumerate((Y_UP, Y_DOWN)):
        column = faces[2 + side][FACE_ROWS : FACE_ROWS + CX, :]
        for i, q in enumerate(group):
            cx = LATTICE[q][0]
            halo_y[side * 5 + i] = column if cx == 0 else pltpu.roll(column, cx % CX, 0)

    def pull(z, carry):
        density = None
        momentum = [None, None, None]
        at = pl.ds(pl.multiple_of(z * CX, CX), CX)
        for q in range(19):
            cx, cy, cz = LATTICE[q]
            source = (z - cz) & (NZ - 1)
            value = pops[q, pl.ds(pl.multiple_of(source * CX, CX), CX), :]
            if cx != 0:
                x = 0 if cx > 0 else CX - 1
                side, group = (0, X_UP) if cx > 0 else (1, X_DOWN)
                edge = faces[side][pl.ds(FACE_ROWS + NZ * group.index(q) + source, 1), :]
                value = jnp.where(
                    row16 == x, jnp.broadcast_to(edge, (CX, CY)), pltpu.roll(value, cx % CX, 0)
                )
            if cy != 0:
                side, group, edges = (0, Y_UP, EDGES_UP) if cy > 0 else (1, Y_DOWN, EDGES_DOWN)
                i = group.index(q)
                y = 0 if cy > 0 else CY - 1
                column = pltpu.roll(
                    halo_y[side * 5 + i], (y + 2 * CY - i * NZ - source) & (CY - 1), 1
                )
                if cx != 0:
                    n = [e[0] for e in edges].index(q)
                    corner = faces[2 + side][pl.ds(FACE_ROWS + source, 1), :]
                    corner = pltpu.roll(jnp.broadcast_to(corner, (CX, CY)), (y - 80 - n) % CY, 1)
                    column = jnp.where(row16 == x, corner, column)
                value = jnp.where(lane16 == y, column, pltpu.roll(value, cy % CY, 1))
            read[q, at, :] = value
            density = value if density is None else density + value
            for k, c in enumerate((cx, cy, cz)):
                if c != 0:
                    signed = value if c > 0 else -value
                    momentum[k] = signed if momentum[k] is None else momentum[k] + signed
        inverse = 1.0 / density
        flow[0, at, :] = density
        for k in range(3):
            flow[1 + k, at, :] = momentum[k]
            flow[4 + k, at, :] = momentum[k] * inverse
        return carry

    lax.fori_loop(0, NZ, pull, 0)

    left = lanes((16, 128)) < 64
    for k in range(3):
        for bz in range(2):
            tiles = [
                flow[4 + k, (8 * bz + iz) * CX + 8 * bx : (8 * bz + iz) * CX + 8 * bx + 8, :]
                for bx in range(2)
                for iz in range(8)
            ]
            turn[...] = jnp.concatenate(tiles, axis=0).T
            for j in range(4):
                even = turn[pl.ds(2 * j, 16, stride=8), :]
                odd = turn[pl.ds(2 * j + 1, 16, stride=8), :]
                pairs = (
                    jnp.where(left, even, pltpu.roll(odd, 64, 1)),
                    jnp.where(left, pltpu.roll(even, 64, 1), odd),
                )
                for bx in range(2):
                    base = (bz * 2 + bx) * 16 * 8
                    cells[j, pl.ds(base + k, 16, stride=8), :] = pairs[bx]

    stiff_product(push, guests, stiffness)
    force[...] = jnp.zeros(force.shape, F32)
    speeds[...] = jnp.zeros(speeds.shape, F32)
    for copy in copies:
        copy.wait()

    def sample_own(turn_number, carry):
        slot = order[turn_number]
        for chunk in range(VERT // CHUNK):
            at = slice(chunk * CHUNK, (chunk + 1) * CHUNK)
            table = tables.at[chunk % 2]
            fill_table(table, states, slot, at)
            homes = [
                pl.multiple_of(bricks[0, 0, slot, chunk * PER_CHUNK + b] * 8, 8)
                for b in range(PER_CHUNK)
            ]
            sample_chunk(speeds.at[0], cells, table, slot, at, homes)
        return carry

    def couple_guest(turn_number, carry):
        slot = order[turn_number]
        for chunk in range(VERT // CHUNK):
            at = slice(chunk * CHUNK, (chunk + 1) * CHUNK)
            table = tables.at[chunk % 2]
            fill_table(table, guests, slot, at)
            homes = [
                pl.multiple_of(
                    meta[slot // 2, 4 + slot % 2, chunk * PER_CHUNK + b].astype(jnp.int32) * 8, 8
                )
                for b in range(PER_CHUNK)
            ]
            sample_chunk(speeds.at[1], cells, table, slot, at, homes)
            spread_chunk(force, table, push, slot, at, homes)
        return carry

    stays = [leave[0, 0, slot] == 0 for slot in range(SLOTS)]
    lax.fori_loop(0, list_active(order, stays), sample_own, 0)
    arrives = [meta[slot // 2, 4 + slot % 2, 64] > 0.5 for slot in range(SLOTS)]
    lax.fori_loop(0, list_active(order, arrives), couple_guest, 0)

    row8 = rows((8, VERT))
    for part, (source, flags) in enumerate(((states, stays), (guests, arrives))):
        active = jnp.zeros((8, VERT), jnp.int32)
        for slot, flag in enumerate(flags):
            active = jnp.where(row8 == slot, flag.astype(jnp.int32), active)
        span = slice(8 * part, 8 * part + 8)
        for k in range(3):
            speed = speeds[part, k]
            half = 0.5 * (source[6 + k] + speed)
            vertex[k, span, :] = jnp.where(active == 1, source[k] + half, 0.0)
            vertex[3 + k, span, :] = jnp.where(active == 1, source[3 + k] + half, 0.0)
            vertex[6 + k, span, :] = jnp.where(active == 1, speed, 0.0)
    vertex_copy = pltpu.make_async_copy(vertex, vertex_out.at[0, 0], out_sem.at[4])
    vertex_copy.start()

    for k in range(3):
        for bz in range(2):
            for j in range(4):
                base = bz * 2 * 16 * 8 + k
                zero = pl.ds(base, 16, stride=8)
                one = pl.ds(base + 128, 16, stride=8)
                zero = force[j, zero, :] + own_force[j, zero, :]
                one = force[j, one, :] + own_force[j, one, :]
                turn[pl.ds(2 * j, 16, stride=8), :] = jnp.where(left, zero, pltpu.roll(one, 64, 1))
                turn[pl.ds(2 * j + 1, 16, stride=8), :] = jnp.where(
                    left, pltpu.roll(zero, 64, 1), one
                )
            back = turn[...].T
            for bx in range(2):
                for iz in range(8):
                    first = (8 * bz + iz) * CX + 8 * bx
                    flow[4 + k, first : first + 8, :] = back[(bx * 8 + iz) * 8 : (bx * 8 + iz) * 8 + 8]

    def collide(z, carry):
        at = pl.ds(pl.multiple_of(z * CX, CX), CX)
        density = flow[0, at, :]
        inverse = 1.0 / density
        body = [flow[4 + k, at, :] for k in range(3)]
        speed = [(flow[1 + k, at, :] + 0.5 * body[k]) * inverse for k in range(3)]
        square = speed[0] * speed[0] + speed[1] * speed[1] + speed[2] * speed[2]
        work = speed[0] * body[0] + speed[1] * body[1] + speed[2] * body[2]
        common = density * (1.25 - 1.875 * square) - 1.125 * work
        wall = solid[at, :] == 1
        read[0, at, :] = jnp.where(wall, read[0, at, :], WEIGHTS[0] * common - 0.25 * read[0, at, :])
        steep = 5.625 * density
        slope = 3.75 * density
        for q in range(1, 19, 2):
            along, push_along = None, None
            for c, s, b in zip(LATTICE[q], speed, body):
                if c != 0:
                    s, b = (s, b) if c > 0 else (-s, -b)
                    along = s if along is None else along + s
                    push_along = b if push_along is None else push_along + b
            even = WEIGHTS[q] * (common + along * (steep * along + 3.375 * push_along))
            odd = WEIGHTS[q] * (slope * along + 1.125 * push_along)
            here, there = read[q, at, :], read[q + 1, at, :]
            read[q, at, :] = jnp.where(wall, there, even + odd - 0.25 * here)
            read[q + 1, at, :] = jnp.where(wall, here, even - odd - 0.25 * there)
        return carry

    def ship(part):
        span = slice(part * 64, (part + 1) * 64)
        return pltpu.make_async_copy(
            read.at[:, span, :], pops_out.at[:, span, :], out_sem.at[part]
        )

    for part in range(4):
        lax.fori_loop(part * 4, part * 4 + 4, collide, 0)
        ship(part).start()
    vertex_copy.wait()
    for part in range(4):
        ship(part).wait()


def step(leave, bricks, pops, solid, states, own_force, faces, stiffness):
    return pl.pallas_call(
        step_kernel,
        out_shape=[
            jax.ShapeDtypeStruct((19, NZ * CX, CY), F32),
            jax.ShapeDtypeStruct((1, 1, 9, ALL, VERT), F32),
        ],
        in_specs=[HBM, HBM] + [VMEM] * 9,
        out_specs=[HBM, HBM],
        scratch_shapes=[
            pltpu.VMEM((19, NZ * CX, CY), F32),
            pltpu.VMEM((7, NZ * CX, CY), F32),
            pltpu.VMEM((10, CX, CY), F32),
            pltpu.VMEM((128, 128), F32),
            pltpu.VMEM((4, 512, 128), F32),
            pltpu.VMEM((4, 512, 128), F32),
            pltpu.VMEM((9, SLOTS, VERT), F32),
            pltpu.VMEM((24, VERT), F32),
            pltpu.VMEM((2, 512, CHUNK), BF16),
            pltpu.VMEM((2, 3, SLOTS, VERT), F32),
            pltpu.VMEM((9, ALL, VERT), F32),
            pltpu.SMEM((1, 1, SLOTS), jnp.int32),
            pltpu.SMEM((1, 1, SLOTS, BLOCKS), jnp.int32),
            pltpu.SMEM((4, 8, 128), F32),
            pltpu.SMEM((SLOTS + 1,), jnp.int32),
            pltpu.SemaphoreType.DMA((6,)),
            pltpu.SemaphoreType.DMA((5,)),
        ],
        compiler_params=pltpu.CompilerParams(vmem_limit_bytes=24 << 20),
        cost_estimate=pl.CostEstimate(
            flops=2 * 10**9, bytes_accessed=10**7, transcendentals=0
        ),
        name="lattice_step",
    )(leave, bricks, pops, solid, states, own_force, *faces, stiffness)


def along_axis(x, axis, by):
    size = lax.axis_size(axis)
    return lax.ppermute(x, axis, [(i, (i + by) % size) for i in range(size)])


def local(populations, solid_mask, bead_states, bead_bricks, leave_dir, stiffness):
    pops = populations.reshape(19, NZ * CX, CY)
    solid = solid_mask.reshape(NZ * CX, CY)
    states = bead_states.transpose(0, 1, 3, 2, 4)
    x_up, x_down = pack_x(leave_dir, bead_bricks, states, populations)
    x_low = along_axis(x_up, "gx", 1)
    x_high = along_axis(x_down, "gx", -1)
    y_up, y_down = pack_y(leave_dir, bead_bricks, states, populations)
    y_up, y_down = add_edges(y_up, y_down, x_low, x_high)
    y_low = along_axis(y_up, "gy", 1)
    y_high = along_axis(y_down, "gy", -1)
    own_force = spread_own(leave_dir, bead_bricks, states, stiffness)
    pops_out, vertex_out = step(
        leave_dir, bead_bricks, pops, solid, states, own_force,
        (x_low, x_high, y_low, y_high), stiffness,
    )
    return (pops_out.reshape(populations.shape), vertex_out.transpose(0, 1, 3, 2, 4))


def solution(mesh):
    return jax.shard_map(
        local,
        mesh=mesh,
        in_specs=(
            P(None, None, "gx", "gy"),
            P(None, "gx", "gy"),
            P("gx", "gy", None, None, None),
            P("gx", "gy", None, None),
            P("gx", "gy", None),
            P(),
        ),
        out_specs=(P(None, None, "gx", "gy"), P("gx", "gy", None, None, None)),
        check_vma=False,
    )
```

time: 63.2 us -> 35.6 us (0.56); the launches traced: 63 us -> 36.3 us
  waiting for transfers between devices: 22.5 us -> 8.13 us
  starting transfers between devices: 19.6 us -> 9.91 us
  local copies, waits for them, and re-layouts: 5.52 us -> 0.03 us
  Pallas kernels: 14.7 us -> 17.4 us
    ppermute x4 -> x0, waiting for transfers between devices: 22.5 us -> none  [across(): return lax.ppermute(x, ('gx', 'gy'), pairs)]
    ppermute x4 -> x0, starting transfers between devices: 11.2 us -> none  [across(): return lax.ppermute(x, ('gx', 'gy'), pairs)]
    ppermute x4, waiting for transfers between devices: 0.01 us -> 8.13 us  [along_axis(): return lax.ppermute(x, axis, [(i, (i + by) % size) for i in range(size)])]
    unnamed x16 -> x12, local copies, waits for them, and re-layouts: 5.52 us -> 0.03 us
    pallas_call x1 -> x4, Pallas kernels: 0.97 us -> 6.42 us  [the longest x1 2.92 us: spread_own(): pl.pallas_call(own_kernel, out_shape=jax.ShapeDtypeStruct((4, 512, 128),...]
    pallas_call x1, Pallas kernels: 13.7 us -> 11 us  [step(): pl.pallas_call(step_kernel, out_shape=[jax.ShapeDtypeStruct((19, NZ * CX,...]
    ppermute x4, starting transfers between devices: 8.33 us -> 9.91 us  [along_axis(): return lax.ppermute(x, axis, [(i, (i + by) % size) for i in range(size)])]
  transfers between devices with their start and end apart: 8 -> 4, of which waited for: 4 -> 2; matrix products, arithmetic and copies ran while one was open for 0% -> 0% of each run, Pallas kernels for 0% -> 11%
where the time goes in v1:
time: 35.6 us; the launch traced here: 36.3 us
  Pallas kernels  17.4 us (49%)
  starting transfers between devices  9.91 us (28%)
  waiting for transfers between devices  8.13 us (23%)
  between operations  0.74 us (2%)
    pallas_call x1, Pallas kernels, step(): pl.pallas_call(step_kernel, out_shape=[jax.ShapeDtypeStruct((19, NZ * CX,...  11 us
    ppermute x4, starting transfers between devices, along_axis(): return lax.ppermute(x, axis, [(i, (i + by) % size) for i in range(size)])  9.91 us
    ppermute x4, waiting for transfers between devices, along_axis(): return lax.ppermute(x, axis, [(i, (i + by) % size) for i in range(size)])  8.13 us
    pallas_call x1, Pallas kernels, spread_own(): pl.pallas_call(own_kernel, out_shape=jax.ShapeDtypeStruct((4, 512, 128),...  2.92 us
    pallas_call x1, Pallas kernels, pack_x(): pl.pallas_call(pack_x_kernel, out_shape=[jax.ShapeDtypeStruct((X_ROWS, 12...  2.24 us
    pallas_call x1, Pallas kernels, pack_y(): pl.pallas_call(pack_y_kernel, out_shape=[jax.ShapeDtypeStruct((Y_ROWS, 12...  1.19 us
  transfers between devices with their start and end apart: 4, of which 2 were waited for; matrix products, arithmetic and copies ran while one was open for 0% of the time, Pallas kernels for 11%

profile of v1, /device:TPU:71, one launch (start us, length us, event | category | flops | bytes accessed | tf_op | source)
XLA Modules:
  0.0 36.3 jit_solution(18261419048667965793)
XLA Ops:
  0.6 0.0 copy-start.5
  0.6 0.0 copy-start.4
  0.7 0.0 copy-start
  0.7 0.0 copy-start.1
  0.7 2.2 %pack_x.1 = (f32[264,128]{1,0:T(8,128)}, f32[264,128]{1,0:T(8,128)}) custom-call(s32[1,1,8]{2,1,0:T(1,128)} %leave_hbm.7, s32[1,1,8,20]{3,2,1,0:T(8,128)} %bricks_hbm.7, f32[1,1,9,8,1280]{4,3,2,1,0:T(8,128)} %bitcast.6, f32[19,16,16,128]{3,2,1,0:T(8,128)} %pops_hbm.3), custom_call_target="tpu_custom_call" | custom-call | flops 1000000 | bytes 1000000 | tf_op jit(solution)/shard_map/pack_x/pallas_call | solution.py:173
  2.9 0.0 copy-start.2
  2.9 4.8 %collective-permute-start = (f32[264,128]{1,0:T(8,128)}, f32[264,128]{1,0:T(8,128)S(1)}, u32[]{:S(2)}, u32[]{:S(2)}) collective-permute-start(f32[264,128]{1,0:T(8,128)} %get-tuple-element.10), channel_id=1, source_target_pairs={{0,8},{8,16},{16,24},{24,32},{32,40},{40,48},{48,56},{56,64},{64,7... | collective-permute-start | bytes 405512 | tf_op jit(solution)/shard_map/ppermute | solution.py:604
  7.7 0.0 collective-permute-start.1
  7.7 0.0 copy-done.5
  7.7 0.0 copy-done.4
  7.7 0.0 copy-done
  7.7 0.0 copy-done.1
  7.7 1.2 %pack_y.1 = (f32[200,128]{1,0:T(8,128)S(1)}, f32[200,128]{1,0:T(8,128)S(1)}) custom-call(s32[1,1,8]{2,1,0:T(1,128)S(1)} %copy-done.5, s32[1,1,8,20]{3,2,1,0:T(8,128)S(1)} %copy-done.4, f32[1,1,9,8,1280]{4,3,2,1,0:T(8,128)S(1)} %bitcast.7, f32[19,16,16,128]{3,2,1,0:T(8,128)S(1)} %copy-done), custom_call_target="tpu_custom_call" | custom-call | flops 1000000 | bytes 2000000 | tf_op jit(solution)/shard_map/pack_y/pallas_call | solution.py:187
  8.9 1.9 %collective-permute-done.x_low = f32[264,128]{1,0:T(8,128)S(1)} collective-permute-done((f32[264,128]{1,0:T(8,128)}, f32[264,128]{1,0:T(8,128)S(1)}, u32[]{:S(2)}, u32[]{:S(2)}) %collective-permute-start) | collective-permute-done | bytes 135200 | tf_op jit(solution)/shard_map/ppermute | solution.py:604
  10.8 6.3 %collective-permute-done.1.x_high = f32[264,128]{1,0:T(8,128)S(1)} collective-permute-done((f32[264,128]{1,0:T(8,128)}, f32[264,128]{1,0:T(8,128)S(1)}, u32[]{:S(2)}, u32[]{:S(2)}) %collective-permute-start.1) | collective-permute-done | bytes 135200 | tf_op jit(solution)/shard_map/ppermute | solution.py:604
  17.0 0.1 add_edges.1
  17.1 2.2 %collective-permute-start.2 = (f32[200,128]{1,0:T(8,128)S(1)}, f32[200,128]{1,0:T(8,128)S(1)}, u32[]{:S(2)}, u32[]{:S(2)}) collective-permute-start(f32[200,128]{1,0:T(8,128)S(1)} %get-tuple-element.14), channel_id=1, source_target_pairs={{0,1},{1,2},{2,3},{3,4},{4,5},{5,6},{6,7},{7,0},{8,9},{9,10},{10,1... | collective-permute-start | bytes 307208 | tf_op jit(solution)/shard_map/ppermute | solution.py:604
  19.3 0.0 copy-start.3
  19.3 2.9 %collective-permute-start.3 = (f32[200,128]{1,0:T(8,128)S(1)}, f32[200,128]{1,0:T(8,128)S(1)}, u32[]{:S(2)}, u32[]{:S(2)}) collective-permute-start(f32[200,128]{1,0:T(8,128)S(1)} %get-tuple-element.15), channel_id=1, source_target_pairs={{0,7},{1,0},{2,1},{3,2},{4,3},{5,4},{6,5},{7,6},{8,15},{9,8},{10,9... | collective-permute-start | bytes 307208 | tf_op jit(solution)/shard_map/ppermute | solution.py:604
  22.3 0.0 copy-done.2
  22.3 2.9 %spread_own.1.own_force = f32[4,512,128]{2,1,0:T(8,128)S(1)} custom-call(s32[1,1,8]{2,1,0:T(1,128)S(1)} %copy-done.5, s32[1,1,8,20]{3,2,1,0:T(8,128)S(1)} %copy-done.4, f32[1,1,9,8,1280]{4,3,2,1,0:T(8,128)S(1)} %bitcast.8, bf16[1280,1280]{1,0:T(8,128)(2,1)S(1)} %copy-done.2), custom_call_target="tpu_custom_call" | custom-call | flops 2000000000 | bytes 5000000 | tf_op jit(solution)/shard_map/spread_own/pallas_call | solution.py:333
  25.2 0.0 collective-permute-done.2.y_low
  25.2 0.0 collective-permute-done.3.y_high
  25.2 0.0 copy-done.3
  25.2 11.0 %lattice_step.1 = (f32[19,256,128]{2,1,0:T(8,128)}, f32[1,1,9,16,1280]{4,3,2,1,0:T(8,128)}) custom-call(s32[1,1,8]{2,1,0:T(1,128)S(1)} %copy-done.5, s32[1,1,8,20]{3,2,1,0:T(8,128)S(1)} %copy-done.4, f32[19,256,128]{2,1,0:T(8,128)S(1)} %bitcast.5, s32[256,128]{1,0:T(8,128)S(1)} %bitcast.10, f32[1,1,9,8,1280]{4,3,2,1,0:T(8,128)S(1)} %bitcast.9, ...), custom_call_target="tpu_custom_call" | custom-call | flops 2000000000 | bytes 10000000 | tf_op jit(solution)/shard_map/lattice_step/pallas_call | solution.py:567
Async XLA Ops:
  0.6 7.1 %copy-start.5 = (s32[1,1,8]{2,1,0:T(1,128)S(1)}, s32[1,1,8]{2,1,0:T(1,128)}, u32[]{:S(2)}) copy-start(s32[1,1,8]{2,1,0:T(1,128)} %leave_hbm.7) | copy-start | bytes 100
  0.6 7.1 %copy-start.4 = (s32[1,1,8,20]{3,2,1,0:T(8,128)S(1)}, s32[1,1,8,20]{3,2,1,0:T(8,128)}, u32[]{:S(2)}) copy-start(s32[1,1,8,20]{3,2,1,0:T(8,128)} %bricks_hbm.7) | copy-start | bytes 1924
  0.7 7.1 %copy-start = (f32[19,16,16,128]{3,2,1,0:T(8,128)S(1)}, f32[19,16,16,128]{3,2,1,0:T(8,128)}, u32[]{:S(2)}) copy-start(f32[19,16,16,128]{3,2,1,0:T(8,128)} %pops_hbm.3) | copy-start | bytes 7471108
  0.7 7.1 %copy-start.1 = (f32[1,1,8,9,1280]{4,2,3,1,0:T(8,128)S(1)}, f32[1,1,8,9,1280]{4,2,3,1,0:T(8,128)}, u32[]{:S(2)}) copy-start(f32[1,1,8,9,1280]{4,2,3,1,0:T(8,128)} %param.8) | copy-start | bytes 1105924
  2.9 19.4 %copy-start.2 = (bf16[1280,1280]{1,0:T(8,128)(2,1)S(1)}, bf16[1280,1280]{1,0:T(8,128)(2,1)}, u32[]{:S(2)}) copy-start(bf16[1280,1280]{1,0:T(8,128)(2,1)} %stiffness.3) | copy-start | bytes 9830404
  2.9 7.8 %collective-permute-start = (f32[264,128]{1,0:T(8,128)}, f32[264,128]{1,0:T(8,128)S(1)}, u32[]{:S(2)}, u32[]{:S(2)}) collective-permute-start(f32[264,128]{1,0:T(8,128)} %get-tuple-element.10), channel_id=1, source_target_pairs={{0,8},{8,16},{16,24},{24,32},{32,40},{40,48},{48,56},{56,64},{64,7... | collective-permute-start | bytes 405512 | tf_op jit(solution)/shard_map/ppermute | solution.py:604
  7.7 9.4 %collective-permute-start.1 = (f32[264,128]{1,0:T(8,128)}, f32[264,128]{1,0:T(8,128)S(1)}, u32[]{:S(2)}, u32[]{:S(2)}) collective-permute-start(f32[264,128]{1,0:T(8,128)} %get-tuple-element.11), channel_id=1, source_target_pairs={{0,248},{8,0},{16,8},{24,16},{32,24},{40,32},{48,40},{56,48},{64,5... | collective-permute-start | bytes 405512 | tf_op jit(solution)/shard_map/ppermute | solution.py:604
  17.1 8.1 %collective-permute-start.2 = (f32[200,128]{1,0:T(8,128)S(1)}, f32[200,128]{1,0:T(8,128)S(1)}, u32[]{:S(2)}, u32[]{:S(2)}) collective-permute-start(f32[200,128]{1,0:T(8,128)S(1)} %get-tuple-element.14), channel_id=1, source_target_pairs={{0,1},{1,2},{2,3},{3,4},{4,5},{5,6},{6,7},{7,0},{8,9},{9,10},{10,1... | collective-permute-start | bytes 307208 | tf_op jit(solution)/shard_map/ppermute | solution.py:604
  19.3 5.9 %copy-start.3 = (s32[16,16,128]{2,1,0:T(8,128)S(1)}, s32[16,16,128]{2,1,0:T(8,128)}, u32[]{:S(2)}) copy-start(s32[16,16,128]{2,1,0:T(8,128)} %param.7) | copy-start | bytes 393220
  19.3 5.9 %collective-permute-start.3 = (f32[200,128]{1,0:T(8,128)S(1)}, f32[200,128]{1,0:T(8,128)S(1)}, u32[]{:S(2)}, u32[]{:S(2)}) collective-permute-start(f32[200,128]{1,0:T(8,128)S(1)} %get-tuple-element.15), channel_id=1, source_target_pairs={{0,7},{1,0},{2,1},{3,2},{4,3},{5,4},{6,5},{7,6},{8,15},{9,8},{10,9... | collective-permute-start | bytes 307208 | tf_op jit(solution)/shard_map/ppermute | solution.py:604

commit v2 on v1

--- a/solution.py
+++ b/solution.py
@@ -52,6 +52,10 @@
 X_ROWS, Y_ROWS = FACE_ROWS + 5 * NZ, FACE_ROWS + CX
 
 
+def parity(axis):
+    return lax.axis_index(axis) & 1
+
+
 def pick(leave, code):
     first, second, count = jnp.int32(0), jnp.int32(0), jnp.int32(0)
     for slot in range(SLOTS):
@@ -86,23 +90,25 @@
 
 
 def pack_x_kernel(
-    leave_hbm, bricks_hbm, states_hbm, pops_hbm, up, down, leave, bricks, states, sem, face_sem
+    leave_hbm, bricks_hbm, states_hbm, pops_hbm, near, far, leave, bricks, states, sem, face_sem
 ):
     copies = fetch_beads(leave_hbm, bricks_hbm, states_hbm, leave, bricks, states, sem)
-    for side, (out, group, x) in enumerate(((up, X_UP, CX - 1), (down, X_DOWN, 0))):
-        for i, q in enumerate(group):
+    near_down = parity("gx")
+    for n, (out, down) in enumerate(((near, near_down), (far, 1 - near_down))):
+        x = (1 - down) * (CX - 1)
+        for i, q in enumerate(X_UP):
             at = FACE_ROWS + NZ * i
             copies.append(
                 pltpu.make_async_copy(
-                    pops_hbm.at[q, :, x, :], out.at[at : at + NZ, :], face_sem.at[side * 5 + i]
+                    pops_hbm.at[q + down, :, x, :], out.at[at : at + NZ, :], face_sem.at[n * 5 + i]
                 )
             )
     for copy in copies:
         copy.start()
     for copy in copies[:3]:
         copy.wait()
-    pack_beads(up, 1, leave, bricks, states)
-    pack_beads(down, 2, leave, bricks, states)
+    pack_beads(near, 1 + near_down, leave, bricks, states)
+    pack_beads(far, 2 - near_down, leave, bricks, states)
     for copy in copies[3:]:
         copy.wait()
 
@@ -112,7 +118,7 @@
 
 
 def pack_y_kernel(
-    leave_hbm, bricks_hbm, states_hbm, pops_hbm, up, down,
+    leave_hbm, bricks_hbm, states_hbm, pops_hbm, near, far,
     leave, bricks, states, pops, sem, pops_sem,
 ):
     copies = fetch_beads(leave_hbm, bricks_hbm, states_hbm, leave, bricks, states, sem)
@@ -127,12 +133,14 @@
         copy.start()
     for copy in copies[:3]:
         copy.wait()
-    pack_beads(up, 3, leave, bricks, states)
-    pack_beads(down, 4, leave, bricks, states)
+    near_down = parity("gy")
+    pack_beads(near, 3 + near_down, leave, bricks, states)
+    pack_beads(far, 4 - near_down, leave, bricks, states)
     for copy in copies[3:]:
         copy.wait()
     lane = lanes((CX, CY))
-    for out, group, y in ((up, Y_UP, CY - 1), (down, Y_DOWN, 0)):
+    columns = []
+    for group, y in ((Y_UP, CY - 1), (Y_DOWN, 0)):
         column = jnp.zeros((CX, CY), F32)
         for i, q in enumerate(group):
             for z in range(NZ):
@@ -140,24 +148,36 @@
                 column = jnp.where(
                     lane == place, pltpu.roll(pops[Y_PLACE[q], z], (place - y) % CY, 1), column
                 )
-        out[FACE_ROWS : FACE_ROWS + CX, :] = column
+        columns.append(column)
+    near[FACE_ROWS : FACE_ROWS + CX, :] = jnp.where(near_down == 1, columns[1], columns[0])
+    far[FACE_ROWS : FACE_ROWS + CX, :] = jnp.where(near_down == 1, columns[0], columns[1])
 
 
 EDGES_UP = ((7, 0), (10, 1))
 EDGES_DOWN = ((9, 0), (8, 1))
 
 
-def edge_kernel(up, down, x_low, x_high, up_out, down_out):
+def edge_kernel(y_near, y_far, x_near, x_far, near_out, far_out):
     lane = lanes((NZ, CY))
-    for source, out, edges, y in ((up, up_out, EDGES_UP, CY - 1), (down, down_out, EDGES_DOWN, 0)):
+    low_is_near = parity("gx") == 1
+    near_down = parity("gy") == 1
+    extra = []
+    for edges, y in ((EDGES_UP, CY - 1), (EDGES_DOWN, 0)):
+        column = jnp.zeros((NZ, CY), F32)
+        for n, (q, side) in enumerate(edges):
+            at = FACE_ROWS + NZ * (X_UP, X_DOWN)[side].index(q)
+            near, far = x_near[at : at + NZ, :], x_far[at : at + NZ, :]
+            face = jnp.where(low_is_near, *((near, far) if side == 0 else (far, near)))
+            column = jnp.where(lane == 80 + n, pltpu.roll(face, (80 + n - y) % CY, 1), column)
+        extra.append(column)
+    up, down = extra
+    for source, out, add in (
+        (y_near, near_out, jnp.where(near_down, down, up)),
+        (y_far, far_out, jnp.where(near_down, up, down)),
+    ):
         out[0:FACE_ROWS, :] = source[0:FACE_ROWS, :]
         column = source[FACE_ROWS : FACE_ROWS + CX, :]
-        for n, (q, side) in enumerate(edges):
-            group, message = ((X_UP, x_low), (X_DOWN, x_high))[side]
-            at = FACE_ROWS + NZ * group.index(q)
-            moved = pltpu.roll(message[at : at + NZ, :], (80 + n - y) % CY, 1)
-            column = jnp.where(lane == 80 + n, moved, column)
-        out[FACE_ROWS : FACE_ROWS + CX, :] = column
+        out[FACE_ROWS : FACE_ROWS + CX, :] = jnp.where(lane < 80, column, add)
 
 
 VMEM = pl.BlockSpec(memory_space=pltpu.VMEM)
@@ -201,7 +221,7 @@
     )(leave, bricks, states, pops)
 
 
-def add_edges(up, down, x_low, x_high):
+def add_edges(y_near, y_far, x_near, x_far):
     return pl.pallas_call(
         edge_kernel,
         out_shape=[jax.ShapeDtypeStruct((Y_ROWS, 128), F32)] * 2,
@@ -209,7 +229,7 @@
         out_specs=[VMEM] * 2,
         compiler_params=pltpu.CompilerParams(vmem_limit_bytes=8 << 20),
         name="add_edges",
-    )(up, down, x_low, x_high)
+    )(y_near, y_far, x_near, x_far)
 
 
 def phi(distance):
@@ -353,13 +373,14 @@
 
 def step_kernel(
     leave_hbm, bricks_hbm, pops, solid, states_in, own_force,
-    x_low, x_high, y_low, y_high,
+    x_near, x_far, y_near, y_far,
     stiffness,
     pops_out, vertex_out,
-    read, flow, halo_y, turn, cells, force, guests, push, tables, speeds, vertex,
+    read, flow, halo_x, halo_y, edges, turn, cells, force, guests, push, tables, speeds, vertex,
     leave, bricks, meta, order, meta_sem, out_sem,
 ):
-    faces = (x_low, x_high, y_low, y_high)
+    faces = (x_near, x_far, y_near, y_far)
+    odd_x, odd_y = parity("gx"), parity("gy")
     states = states_in.at[0, 0]
     copies = [
         pltpu.make_async_copy(faces[side].at[176:184, :], meta.at[side], meta_sem.at[side])
@@ -378,10 +399,17 @@
                     18 * c + 2 * entry : 18 * c + 2 * entry + 2, :
                 ]
 
+    for face, side in ((x_near, 1 - odd_x), (x_far, odd_x)):
+        for i in range(5):
+            at = FACE_ROWS + NZ * i
+            halo_x[side, i] = face[at : at + NZ, :]
     row16 = rows((CX, CY))
     lane16 = lanes((CX, CY))
+    near, far = [face[FACE_ROWS : FACE_ROWS + CX, :] for face in (y_near, y_far)]
+    edges[1 - odd_y] = near
+    edges[odd_y] = far
     for side, group in enumerate((Y_UP, Y_DOWN)):
-        column = faces[2 + side][FACE_ROWS : FACE_ROWS + CX, :]
+        column = jnp.where(odd_y == 1, *((near, far) if side == 0 else (far, near)))
         for i, q in enumerate(group):
             cx = LATTICE[q][0]
             halo_y[side * 5 + i] = column if cx == 0 else pltpu.roll(column, cx % CX, 0)
@@ -397,20 +425,20 @@
             if cx != 0:
                 x = 0 if cx > 0 else CX - 1
                 side, group = (0, X_UP) if cx > 0 else (1, X_DOWN)
-                edge = faces[side][pl.ds(FACE_ROWS + NZ * group.index(q) + source, 1), :]
+                edge = halo_x[side, group.index(q), pl.ds(source, 1), :]
                 value = jnp.where(
                     row16 == x, jnp.broadcast_to(edge, (CX, CY)), pltpu.roll(value, cx % CX, 0)
                 )
             if cy != 0:
-                side, group, edges = (0, Y_UP, EDGES_UP) if cy > 0 else (1, Y_DOWN, EDGES_DOWN)
+                side, group, pair = (0, Y_UP, EDGES_UP) if cy > 0 else (1, Y_DOWN, EDGES_DOWN)
                 i = group.index(q)
                 y = 0 if cy > 0 else CY - 1
                 column = pltpu.roll(
                     halo_y[side * 5 + i], (y + 2 * CY - i * NZ - source) & (CY - 1), 1
                 )
                 if cx != 0:
-                    n = [e[0] for e in edges].index(q)
-                    corner = faces[2 + side][pl.ds(FACE_ROWS + source, 1), :]
+                    n = [e[0] for e in pair].index(q)
+                    corner = edges[side, pl.ds(source, 1), :]
                     corner = pltpu.roll(jnp.broadcast_to(corner, (CX, CY)), (y - 80 - n) % CY, 1)
                     column = jnp.where(row16 == x, corner, column)
                 value = jnp.where(lane16 == y, column, pltpu.roll(value, cy % CY, 1))
@@ -490,18 +518,25 @@
     lax.fori_loop(0, list_active(order, arrives), couple_guest, 0)
 
     row8 = rows((8, VERT))
+
+    def by_side(value):
+        pair = (row8 // 2) & 1
+        turned = jnp.where(pair == 0, pltpu.roll(value, 6, 0), pltpu.roll(value, 2, 0))
+        return jnp.where(jnp.where(row8 < 4, 1 - odd_x, 1 - odd_y) == 1, turned, value)
+
     for part, (source, flags) in enumerate(((states, stays), (guests, arrives))):
         active = jnp.zeros((8, VERT), jnp.int32)
         for slot, flag in enumerate(flags):
             active = jnp.where(row8 == slot, flag.astype(jnp.int32), active)
         span = slice(8 * part, 8 * part + 8)
+        place = by_side if part == 1 else lambda value: value
         for k in range(3):
             speed = speeds[part, k]
             half = 0.5 * (source[6 + k] + speed)
-            vertex[k, span, :] = jnp.where(active == 1, source[k] + half, 0.0)
-            vertex[3 + k, span, :] = jnp.where(active == 1, source[3 + k] + half, 0.0)
-            vertex[6 + k, span, :] = jnp.where(active == 1, speed, 0.0)
-    vertex_copy = pltpu.make_async_copy(vertex, vertex_out.at[0, 0], out_sem.at[4])
+            vertex[k, span, :] = place(jnp.where(active == 1, source[k] + half, 0.0))
+            vertex[3 + k, span, :] = place(jnp.where(active == 1, source[3 + k] + half, 0.0))
+            vertex[6 + k, span, :] = place(jnp.where(active == 1, speed, 0.0))
+    vertex_copy = pltpu.make_async_copy(vertex, vertex_out.at[0, 0], out_sem.at[8])
     vertex_copy.start()
 
     for k in range(3):
@@ -550,16 +585,16 @@
         return carry
 
     def ship(part):
-        span = slice(part * 64, (part + 1) * 64)
+        span = slice(part * 32, (part + 1) * 32)
         return pltpu.make_async_copy(
             read.at[:, span, :], pops_out.at[:, span, :], out_sem.at[part]
         )
 
-    for part in range(4):
-        lax.fori_loop(part * 4, part * 4 + 4, collide, 0)
+    for part in range(8):
+        lax.fori_loop(part * 2, part * 2 + 2, collide, 0)
         ship(part).start()
     vertex_copy.wait()
-    for part in range(4):
+    for part in range(8):
         ship(part).wait()
 
 
@@ -575,7 +610,9 @@
         scratch_shapes=[
             pltpu.VMEM((19, NZ * CX, CY), F32),
             pltpu.VMEM((7, NZ * CX, CY), F32),
+            pltpu.VMEM((2, 5, NZ, CY), F32),
             pltpu.VMEM((10, CX, CY), F32),
+            pltpu.VMEM((2, NZ, CY), F32),
             pltpu.VMEM((128, 128), F32),
             pltpu.VMEM((4, 512, 128), F32),
             pltpu.VMEM((4, 512, 128), F32),
@@ -589,7 +626,7 @@
             pltpu.SMEM((4, 8, 128), F32),
             pltpu.SMEM((SLOTS + 1,), jnp.int32),
             pltpu.SemaphoreType.DMA((6,)),
-            pltpu.SemaphoreType.DMA((5,)),
+            pltpu.SemaphoreType.DMA((9,)),
         ],
         compiler_params=pltpu.CompilerParams(vmem_limit_bytes=24 << 20),
         cost_estimate=pl.CostEstimate(
@@ -599,26 +636,28 @@
     )(leave, bricks, pops, solid, states, own_force, *faces, stiffness)
 
 
-def along_axis(x, axis, by):
+def exchange(x, axis, far):
     size = lax.axis_size(axis)
-    return lax.ppermute(x, axis, [(i, (i + by) % size) for i in range(size)])
+    return lax.ppermute(
+        x, axis, [(i, (i + (1 if i % 2 == far else -1)) % size) for i in range(size)]
+    )
 
 
 def local(populations, solid_mask, bead_states, bead_bricks, leave_dir, stiffness):
     pops = populations.reshape(19, NZ * CX, CY)
     solid = solid_mask.reshape(NZ * CX, CY)
     states = bead_states.transpose(0, 1, 3, 2, 4)
-    x_up, x_down = pack_x(leave_dir, bead_bricks, states, populations)
-    x_low = along_axis(x_up, "gx", 1)
-    x_high = along_axis(x_down, "gx", -1)
-    y_up, y_down = pack_y(leave_dir, bead_bricks, states, populations)
-    y_up, y_down = add_edges(y_up, y_down, x_low, x_high)
-    y_low = along_axis(y_up, "gy", 1)
-    y_high = along_axis(y_down, "gy", -1)
+    x_near, x_far = pack_x(leave_dir, bead_bricks, states, populations)
+    x_far = exchange(x_far, "gx", 1)
+    x_near = exchange(x_near, "gx", 0)
+    y_near, y_far = pack_y(leave_dir, bead_bricks, states, populations)
+    y_near, y_far = add_edges(y_near, y_far, x_near, x_far)
+    y_far = exchange(y_far, "gy", 1)
+    y_near = exchange(y_near, "gy", 0)
     own_force = spread_own(leave_dir, bead_bricks, states, stiffness)
     pops_out, vertex_out = step(
         leave_dir, bead_bricks, pops, solid, states, own_force,
-        (x_low, x_high, y_low, y_high), stiffness,
+        (x_near, x_far, y_near, y_far), stiffness,
     )
     return (pops_out.reshape(populations.shape), vertex_out.transpose(0, 1, 3, 2, 4))
 

time: 35.6 us -> 34 us (0.955)
  the two profiles are of different devices: /device:TPU:71 before, /device:TPU:56 now
where the time goes in v2:
time: 34 us; the launch traced here: 33.7 us
  Pallas kernels  17.7 us (52%)
  starting transfers between devices  9.5 us (28%)
  waiting for transfers between devices  5.72 us (17%)
  between operations  0.73 us (2%)
    pallas_call x1, Pallas kernels, step(): pl.pallas_call(step_kernel, out_shape=[jax.ShapeDtypeStruct((19, NZ * CX,...  10.7 us
    ppermute x4, starting transfers between devices, exchange(): lax.ppermute(x, axis, [(i, (i + (1 if i % 2 == far else -1)) % size) for...  9.5 us
    ppermute x4, waiting for transfers between devices, exchange(): lax.ppermute(x, axis, [(i, (i + (1 if i % 2 == far else -1)) % size) for...  5.72 us
    pallas_call x1, Pallas kernels, spread_own(): pl.pallas_call(own_kernel, out_shape=jax.ShapeDtypeStruct((4, 512, 128),...  3.45 us
    pallas_call x1, Pallas kernels, pack_x(): pl.pallas_call(pack_x_kernel, out_shape=[jax.ShapeDtypeStruct((X_ROWS, 12...  2.25 us
    pallas_call x1, Pallas kernels, pack_y(): pl.pallas_call(pack_y_kernel, out_shape=[jax.ShapeDtypeStruct((Y_ROWS, 12...  1.19 us
  transfers between devices with their start and end apart: 4, of which 2 were waited for; matrix products, arithmetic and copies ran while one was open for 0% of the time, Pallas kernels for 14%

profile of v2, /device:TPU:56, one launch (start us, length us, event | category | flops | bytes accessed | tf_op | source)
XLA Modules:
  0.0 33.7 jit_solution(10803814409727842120)
XLA Ops:
  0.6 0.0 copy-start.5
  0.6 0.0 copy-start.4
  0.7 0.0 copy-start
  0.7 0.0 copy-start.1
  0.7 2.3 %pack_x.1 = (f32[264,128]{1,0:T(8,128)}, f32[264,128]{1,0:T(8,128)}) custom-call(s32[1,1,8]{2,1,0:T(1,128)} %leave_hbm.7, s32[1,1,8,20]{3,2,1,0:T(8,128)} %bricks_hbm.7, f32[1,1,9,8,1280]{4,3,2,1,0:T(8,128)} %bitcast.6, f32[19,16,16,128]{3,2,1,0:T(8,128)} %pops_hbm.3), custom_call_target="tpu_custom_call" | custom-call | flops 1000000 | bytes 1000000 | tf_op jit(solution)/shard_map/pack_x/pallas_call | solution.py:193
  2.9 0.0 copy-start.2
  2.9 0.1 collective-permute-start
  3.0 7.7 %collective-permute-start.1 = (f32[264,128]{1,0:T(8,128)}, f32[264,128]{1,0:T(8,128)S(1)}, u32[]{:S(2)}, u32[]{:S(2)}) collective-permute-start(f32[264,128]{1,0:T(8,128)} %get-tuple-element.11), channel_id=1, source_target_pairs={{0,248},{8,16},{16,8},{24,32},{32,24},{40,48},{48,40},{56,64},{64,... | collective-permute-start | bytes 405512 | tf_op jit(solution)/shard_map/ppermute | solution.py:641
  10.7 0.0 copy-done.5
  10.7 0.0 copy-done.4
  10.7 0.0 copy-done
  10.8 0.0 copy-done.1
  10.8 1.2 %pack_y.1 = (f32[200,128]{1,0:T(8,128)S(1)}, f32[200,128]{1,0:T(8,128)S(1)}) custom-call(s32[1,1,8]{2,1,0:T(1,128)S(1)} %copy-done.5, s32[1,1,8,20]{3,2,1,0:T(8,128)S(1)} %copy-done.4, f32[1,1,9,8,1280]{4,3,2,1,0:T(8,128)S(1)} %bitcast.7, f32[19,16,16,128]{3,2,1,0:T(8,128)S(1)} %copy-done), custom_call_target="tpu_custom_call" | custom-call | flops 1000000 | bytes 2000000 | tf_op jit(solution)/shard_map/pack_y/pallas_call | solution.py:207
  12.0 0.0 collective-permute-done.x_near
  12.0 3.2 %collective-permute-done.1.x_far = f32[264,128]{1,0:T(8,128)S(1)} collective-permute-done((f32[264,128]{1,0:T(8,128)}, f32[264,128]{1,0:T(8,128)S(1)}, u32[]{:S(2)}, u32[]{:S(2)}) %collective-permute-start.1) | collective-permute-done | bytes 135200 | tf_op jit(solution)/shard_map/ppermute | solution.py:641
  15.2 0.1 add_edges.1
  15.3 0.9 %collective-permute-start.2 = (f32[200,128]{1,0:T(8,128)S(1)}, f32[200,128]{1,0:T(8,128)S(1)}, u32[]{:S(2)}, u32[]{:S(2)}) collective-permute-start(f32[200,128]{1,0:T(8,128)S(1)} %get-tuple-element.14), channel_id=1, source_target_pairs={{0,1},{1,0},{2,3},{3,2},{4,5},{5,4},{6,7},{7,6},{8,9},{9,8},{10,11... | collective-permute-start | bytes 307208 | tf_op jit(solution)/shard_map/ppermute | solution.py:641
  16.2 0.0 copy-start.3
  16.2 0.8 %collective-permute-start.3 = (f32[200,128]{1,0:T(8,128)S(1)}, f32[200,128]{1,0:T(8,128)S(1)}, u32[]{:S(2)}, u32[]{:S(2)}) collective-permute-start(f32[200,128]{1,0:T(8,128)S(1)} %get-tuple-element.15), channel_id=1, source_target_pairs={{0,7},{1,2},{2,1},{3,4},{4,3},{5,6},{6,5},{7,0},{8,15},{9,10},{10,... | collective-permute-start | bytes 307208 | tf_op jit(solution)/shard_map/ppermute | solution.py:641
  17.0 0.0 copy-done.2
  17.0 3.5 %spread_own.1.own_force = f32[4,512,128]{2,1,0:T(8,128)S(1)} custom-call(s32[1,1,8]{2,1,0:T(1,128)S(1)} %copy-done.5, s32[1,1,8,20]{3,2,1,0:T(8,128)S(1)} %copy-done.4, f32[1,1,9,8,1280]{4,3,2,1,0:T(8,128)S(1)} %bitcast.8, bf16[1280,1280]{1,0:T(8,128)(2,1)S(1)} %copy-done.2), custom_call_target="tpu_custom_call" | custom-call | flops 2000000000 | bytes 5000000 | tf_op jit(solution)/shard_map/spread_own/pallas_call | solution.py:353
  20.5 0.0 collective-permute-done.2.y_near
  20.5 2.5 %collective-permute-done.3.y_far = f32[200,128]{1,0:T(8,128)S(1)} collective-permute-done((f32[200,128]{1,0:T(8,128)S(1)}, f32[200,128]{1,0:T(8,128)S(1)}, u32[]{:S(2)}, u32[]{:S(2)}) %collective-permute-start.3) | collective-permute-done | bytes 102432 | tf_op jit(solution)/shard_map/ppermute | solution.py:641
  23.0 0.0 copy-done.3
  23.0 10.7 %lattice_step.1 = (f32[19,256,128]{2,1,0:T(8,128)}, f32[1,1,9,16,1280]{4,3,2,1,0:T(8,128)}) custom-call(s32[1,1,8]{2,1,0:T(1,128)S(1)} %copy-done.5, s32[1,1,8,20]{3,2,1,0:T(8,128)S(1)} %copy-done.4, f32[19,256,128]{2,1,0:T(8,128)S(1)} %bitcast.5, s32[256,128]{1,0:T(8,128)S(1)} %bitcast.10, f32[1,1,9,8,1280]{4,3,2,1,0:T(8,128)S(1)} %bitcast.9, ...), custom_call_target="tpu_custom_call" | custom-call | flops 2000000000 | bytes 10000000 | tf_op jit(solution)/shard_map/lattice_step/pallas_call | solution.py:602
Async XLA Ops:
  0.6 10.1 %copy-start.5 = (s32[1,1,8]{2,1,0:T(1,128)S(1)}, s32[1,1,8]{2,1,0:T(1,128)}, u32[]{:S(2)}) copy-start(s32[1,1,8]{2,1,0:T(1,128)} %leave_hbm.7) | copy-start | bytes 100
  0.6 10.1 %copy-start.4 = (s32[1,1,8,20]{3,2,1,0:T(8,128)S(1)}, s32[1,1,8,20]{3,2,1,0:T(8,128)}, u32[]{:S(2)}) copy-start(s32[1,1,8,20]{3,2,1,0:T(8,128)} %bricks_hbm.7) | copy-start | bytes 1924
  0.7 10.1 %copy-start = (f32[19,16,16,128]{3,2,1,0:T(8,128)S(1)}, f32[19,16,16,128]{3,2,1,0:T(8,128)}, u32[]{:S(2)}) copy-start(f32[19,16,16,128]{3,2,1,0:T(8,128)} %pops_hbm.3) | copy-start | bytes 7471108
  0.7 10.1 %copy-start.1 = (f32[1,1,8,9,1280]{4,2,3,1,0:T(8,128)S(1)}, f32[1,1,8,9,1280]{4,2,3,1,0:T(8,128)}, u32[]{:S(2)}) copy-start(f32[1,1,8,9,1280]{4,2,3,1,0:T(8,128)} %param.8) | copy-start | bytes 1105924
  2.9 14.1 %copy-start.2 = (bf16[1280,1280]{1,0:T(8,128)(2,1)S(1)}, bf16[1280,1280]{1,0:T(8,128)(2,1)}, u32[]{:S(2)}) copy-start(bf16[1280,1280]{1,0:T(8,128)(2,1)} %stiffness.3) | copy-start | bytes 9830404
  2.9 9.0 %collective-permute-start = (f32[264,128]{1,0:T(8,128)}, f32[264,128]{1,0:T(8,128)S(1)}, u32[]{:S(2)}, u32[]{:S(2)}) collective-permute-start(f32[264,128]{1,0:T(8,128)} %get-tuple-element.10), channel_id=1, source_target_pairs={{0,8},{8,0},{16,24},{24,16},{32,40},{40,32},{48,56},{56,48},{64,72... | collective-permute-start | bytes 405512 | tf_op jit(solution)/shard_map/ppermute | solution.py:641
  3.0 12.2 %collective-permute-start.1 = (f32[264,128]{1,0:T(8,128)}, f32[264,128]{1,0:T(8,128)S(1)}, u32[]{:S(2)}, u32[]{:S(2)}) collective-permute-start(f32[264,128]{1,0:T(8,128)} %get-tuple-element.11), channel_id=1, source_target_pairs={{0,248},{8,16},{16,8},{24,32},{32,24},{40,48},{48,40},{56,64},{64,... | collective-permute-start | bytes 405512 | tf_op jit(solution)/shard_map/ppermute | solution.py:641
  15.3 5.2 %collective-permute-start.2 = (f32[200,128]{1,0:T(8,128)S(1)}, f32[200,128]{1,0:T(8,128)S(1)}, u32[]{:S(2)}, u32[]{:S(2)}) collective-permute-start(f32[200,128]{1,0:T(8,128)S(1)} %get-tuple-element.14), channel_id=1, source_target_pairs={{0,1},{1,0},{2,3},{3,2},{4,5},{5,4},{6,7},{7,6},{8,9},{9,8},{10,11... | collective-permute-start | bytes 307208 | tf_op jit(solution)/shard_map/ppermute | solution.py:641
  16.2 6.8 %copy-start.3 = (s32[16,16,128]{2,1,0:T(8,128)S(1)}, s32[16,16,128]{2,1,0:T(8,128)}, u32[]{:S(2)}) copy-start(s32[16,16,128]{2,1,0:T(8,128)} %param.7) | copy-start | bytes 393220
  16.2 6.8 %collective-permute-start.3 = (f32[200,128]{1,0:T(8,128)S(1)}, f32[200,128]{1,0:T(8,128)S(1)}, u32[]{:S(2)}, u32[]{:S(2)}) collective-permute-start(f32[200,128]{1,0:T(8,128)S(1)} %get-tuple-element.15), channel_id=1, source_target_pairs={{0,7},{1,2},{2,1},{3,4},{4,3},{5,6},{6,5},{7,0},{8,15},{9,10},{10,... | collective-permute-start | bytes 307208 | tf_op jit(solution)/shard_map/ppermute | solution.py:641

commit v3 on v2

--- a/solution.py
+++ b/solution.py
@@ -197,7 +197,7 @@
         out_specs=[VMEM] * 2,
         scratch_shapes=BEAD_SCRATCH
         + [pltpu.SemaphoreType.DMA((3,)), pltpu.SemaphoreType.DMA((10,))],
-        compiler_params=pltpu.CompilerParams(vmem_limit_bytes=60 << 20),
+        compiler_params=pltpu.CompilerParams(vmem_limit_bytes=62 << 20),
         cost_estimate=pl.CostEstimate(flops=10**6, bytes_accessed=10**6, transcendentals=0),
         name="pack_x",
     )(leave, bricks, states, pops)
@@ -275,7 +275,7 @@
         push[:, at] = -jnp.dot(shape, stiffness[:, at], preferred_element_type=F32)
 
 
-def spread_chunk(force, table, push, slot, at, homes):
+def spread_product(table, push, slot, at):
     row8 = rows((8, CHUNK))
     block = lanes((8, CHUNK)) // 64
     parts = [
@@ -285,16 +285,18 @@
     drives = jnp.concatenate(
         [jnp.where(block == b, drive, 0.0) for b in range(PER_CHUNK)], axis=0
     ).astype(BF16)
-    spread = lax.dot_general(
+    return lax.dot_general(
         drives, table[...], (((1,), (1,)), ((), ())), preferred_element_type=F32
     )
+
+
+def spread_finish(force, spread, homes):
     for b, home in enumerate(homes):
         for j in range(4):
             force[j, pl.ds(home, 8), :] += spread[8 * b : 8 * b + 8, 128 * j : 128 * j + 128]
 
 
-def sample_chunk(sampled_speed, cells, table, slot, at, homes):
-    block = lanes((8, CHUNK)) // 64
+def sample_product(cells, table, homes):
     nearby = jnp.concatenate(
         [
             jnp.concatenate([cells[j, pl.ds(home, 8), :] for j in range(4)], axis=1)
@@ -302,12 +304,19 @@
         ],
         axis=0,
     ).astype(BF16)
-    sampled = jnp.dot(nearby, table[...], preferred_element_type=F32)
+    return jnp.dot(nearby, table[...], preferred_element_type=F32)
+
+
+def sample_finish(sampled_speed, sampled, slot, at):
+    block = lanes((8, CHUNK)) // 64
     speed = sampled[0:8]
     for b in range(1, PER_CHUNK):
         speed = jnp.where(block == b, sampled[8 * b : 8 * b + 8], speed)
     for k in range(3):
         sampled_speed[k, pl.ds(slot, 1), at] = speed[k : k + 1, :]
+
+
+CHUNKS = [slice(n * CHUNK, (n + 1) * CHUNK) for n in range(VERT // CHUNK)]
 
 
 def list_active(order, flags):
@@ -335,15 +344,15 @@
 
     def couple(turn_number, carry):
         slot = order[turn_number]
-        for chunk in range(VERT // CHUNK):
-            at = slice(chunk * CHUNK, (chunk + 1) * CHUNK)
-            table = tables.at[chunk % 2]
-            fill_table(table, states.at[0, 0], slot, at)
+        for n, at in enumerate(CHUNKS):
+            fill_table(tables.at[n], states.at[0, 0], slot, at)
+        spreads = [spread_product(tables.at[n], push, slot, at) for n, at in enumerate(CHUNKS)]
+        for n, spread in enumerate(spreads):
             homes = [
-                pl.multiple_of(bricks[0, 0, slot, chunk * PER_CHUNK + b] * 8, 8)
+                pl.multiple_of(bricks[0, 0, slot, n * PER_CHUNK + b] * 8, 8)
                 for b in range(PER_CHUNK)
             ]
-            spread_chunk(force, table, push, slot, at, homes)
+            spread_finish(force, spread, homes)
         return carry
 
     lax.fori_loop(0, count, couple, 0)
@@ -359,7 +368,7 @@
             pltpu.SMEM((1, 1, SLOTS), jnp.int32),
             pltpu.SMEM((1, 1, SLOTS, BLOCKS), jnp.int32),
             pltpu.VMEM((24, VERT), F32),
-            pltpu.VMEM((2, 512, CHUNK), BF16),
+            pltpu.VMEM((VERT // CHUNK, 512, CHUNK), BF16),
             pltpu.SMEM((SLOTS + 1,), jnp.int32),
             pltpu.SemaphoreType.DMA((2,)),
         ],
@@ -455,7 +464,7 @@
             flow[4 + k, at, :] = momentum[k] * inverse
         return carry
 
-    lax.fori_loop(0, NZ, pull, 0)
+    lax.fori_loop(0, NZ, pull, 0, unroll=True)
 
     left = lanes((16, 128)) < 64
     for k in range(3):
@@ -485,31 +494,39 @@
 
     def sample_own(turn_number, carry):
         slot = order[turn_number]
-        for chunk in range(VERT // CHUNK):
-            at = slice(chunk * CHUNK, (chunk + 1) * CHUNK)
-            table = tables.at[chunk % 2]
-            fill_table(table, states, slot, at)
+        for n, at in enumerate(CHUNKS):
+            fill_table(tables.at[n], states, slot, at)
+        products = []
+        for n in range(len(CHUNKS)):
             homes = [
-                pl.multiple_of(bricks[0, 0, slot, chunk * PER_CHUNK + b] * 8, 8)
+                pl.multiple_of(bricks[0, 0, slot, n * PER_CHUNK + b] * 8, 8)
                 for b in range(PER_CHUNK)
             ]
-            sample_chunk(speeds.at[0], cells, table, slot, at, homes)
+            products.append(sample_product(cells, tables.at[n], homes))
+        for product, at in zip(products, CHUNKS):
+            sample_finish(speeds.at[0], product, slot, at)
         return carry
 
     def couple_guest(turn_number, carry):
         slot = order[turn_number]
-        for chunk in range(VERT // CHUNK):
-            at = slice(chunk * CHUNK, (chunk + 1) * CHUNK)
-            table = tables.at[chunk % 2]
-            fill_table(table, guests, slot, at)
-            homes = [
+        for n, at in enumerate(CHUNKS):
+            fill_table(tables.at[n], guests, slot, at)
+        homes = [
+            [
                 pl.multiple_of(
-                    meta[slot // 2, 4 + slot % 2, chunk * PER_CHUNK + b].astype(jnp.int32) * 8, 8
+                    meta[slot // 2, 4 + slot % 2, n * PER_CHUNK + b].astype(jnp.int32) * 8, 8
                 )
                 for b in range(PER_CHUNK)
             ]
-            sample_chunk(speeds.at[1], cells, table, slot, at, homes)
-            spread_chunk(force, table, push, slot, at, homes)
+            for n in range(len(CHUNKS))
+        ]
+        products = [
+            (sample_product(cells, tables.at[n], homes[n]), spread_product(tables.at[n], push, slot, at))
+            for n, at in enumerate(CHUNKS)
+        ]
+        for n, at in enumerate(CHUNKS):
+            sample_finish(speeds.at[1], products[n][0], slot, at)
+            spread_finish(force, products[n][1], homes[n])
         return carry
 
     stays = [leave[0, 0, slot] == 0 for slot in range(SLOTS)]
@@ -618,7 +635,7 @@
             pltpu.VMEM((4, 512, 128), F32),
             pltpu.VMEM((9, SLOTS, VERT), F32),
             pltpu.VMEM((24, VERT), F32),
-            pltpu.VMEM((2, 512, CHUNK), BF16),
+            pltpu.VMEM((VERT // CHUNK, 512, CHUNK), BF16),
             pltpu.VMEM((2, 3, SLOTS, VERT), F32),
             pltpu.VMEM((9, ALL, VERT), F32),
             pltpu.SMEM((1, 1, SLOTS), jnp.int32),

time: 34 us -> 32.1 us (0.944); the launches traced: 33.7 us -> 32.4 us
  waiting for transfers between devices: 5.72 us -> 3.49 us
  local copies, waits for them, and re-layouts: 0.03 us -> 1.72 us
  Pallas kernels: 17.7 us -> 17 us
    ppermute x4, waiting for transfers between devices: 5.72 us -> 3.49 us  [exchange(): lax.ppermute(x, axis, [(i, (i + (1 if i % 2 == far else -1)) % size) for...]
    unnamed x12 -> x14, local copies, waits for them, and re-layouts: 0.03 us -> 1.72 us
    pallas_call x1, Pallas kernels: 10.7 us -> 9.53 us  [step(): pl.pallas_call(step_kernel, out_shape=[jax.ShapeDtypeStruct((19, NZ * CX,...]
    pallas_call x1, Pallas kernels: 3.45 us -> 3.99 us  [spread_own(): pl.pallas_call(own_kernel, out_shape=jax.ShapeDtypeStruct((4, 512, 128),...]
  transfers between devices with their start and end apart: 4 -> 4, of which waited for: 2 -> 2; matrix products, arithmetic and copies ran while one was open for 0% -> 0% of each run, Pallas kernels for 14% -> 16%
where the time goes in v3:
time: 32.1 us; the launch traced here: 32.4 us
  Pallas kernels  17 us (53%)
  starting transfers between devices  9.5 us (30%)
  waiting for transfers between devices  3.49 us (11%)
  local copies, waits for them, and re-layouts  1.72 us (5%)
  between operations  0.72 us (2%)
    pallas_call x1, Pallas kernels, step(): pl.pallas_call(step_kernel, out_shape=[jax.ShapeDtypeStruct((19, NZ * CX,...  9.53 us
    ppermute x4, starting transfers between devices, exchange(): lax.ppermute(x, axis, [(i, (i + (1 if i % 2 == far else -1)) % size) for...  9.5 us
    pallas_call x1, Pallas kernels, spread_own(): pl.pallas_call(own_kernel, out_shape=jax.ShapeDtypeStruct((4, 512, 128),...  3.99 us
    ppermute x4, waiting for transfers between devices, exchange(): lax.ppermute(x, axis, [(i, (i + (1 if i % 2 == far else -1)) % size) for...  3.49 us
    pallas_call x1, Pallas kernels, pack_x(): pl.pallas_call(pack_x_kernel, out_shape=[jax.ShapeDtypeStruct((X_ROWS, 12...  2.17 us
    unnamed x14, local copies, waits for them, and re-layouts  1.72 us
    pallas_call x1, Pallas kernels, pack_y(): pl.pallas_call(pack_y_kernel, out_shape=[jax.ShapeDtypeStruct((Y_ROWS, 12...  1.19 us
  transfers between devices with their start and end apart: 4, of which 2 were waited for; matrix products, arithmetic and copies ran while one was open for 0% of the time, Pallas kernels for 16%

profile of v3, /device:TPU:56, one launch (start us, length us, event | category | flops | bytes accessed | tf_op | source)
XLA Modules:
  0.0 32.4 jit_solution(1270858802512139250)
XLA Ops:
  0.6 0.0 copy-start.6
  0.6 0.0 copy-start.5
  0.7 0.0 copy-start.2
  0.7 2.2 %pack_x.1 = (f32[264,128]{1,0:T(8,128)}, f32[264,128]{1,0:T(8,128)}) custom-call(s32[1,1,8]{2,1,0:T(1,128)} %leave_hbm.7, s32[1,1,8,20]{3,2,1,0:T(8,128)} %bricks_hbm.7, f32[1,1,9,8,1280]{4,3,2,1,0:T(8,128)} %bitcast.6, f32[19,16,16,128]{3,2,1,0:T(8,128)} %pops_hbm.3), custom_call_target="tpu_custom_call" | custom-call | flops 1000000 | bytes 1000000 | tf_op jit(solution)/shard_map/pack_x/pallas_call | solution.py:193
  2.8 0.1 collective-permute-start
  2.9 7.7 %collective-permute-start.1 = (f32[264,128]{1,0:T(8,128)}, f32[264,128]{1,0:T(8,128)S(1)}, u32[]{:S(2)}, u32[]{:S(2)}) collective-permute-start(f32[264,128]{1,0:T(8,128)} %get-tuple-element.11), channel_id=1, source_target_pairs={{0,248},{8,16},{16,8},{24,32},{32,24},{40,48},{48,40},{56,64},{64,... | collective-permute-start | bytes 405512 | tf_op jit(solution)/shard_map/ppermute | solution.py:658
  10.6 0.0 copy-done.6
  10.6 0.0 copy-done.5
  10.6 0.0 copy-done.2
  10.6 0.0 copy-start
  10.6 1.7 %copy-done = f32[19,16,16,128]{3,2,1,0:T(8,128)S(1)} copy-done((f32[19,16,16,128]{3,2,1,0:T(8,128)S(1)}, f32[19,16,16,128]{3,2,1,0:T(8,128)}, u32[]{:S(2)}) %copy-start) | copy-done | bytes 2490392
  12.3 0.0 copy-start.3
  12.3 1.2 %pack_y.1 = (f32[200,128]{1,0:T(8,128)S(1)}, f32[200,128]{1,0:T(8,128)S(1)}) custom-call(s32[1,1,8]{2,1,0:T(1,128)S(1)} %copy-done.6, s32[1,1,8,20]{3,2,1,0:T(8,128)S(1)} %copy-done.5, f32[1,1,9,8,1280]{4,3,2,1,0:T(8,128)S(1)} %bitcast.7, f32[19,16,16,128]{3,2,1,0:T(8,128)S(1)} %copy-done), custom_call_target="tpu_custom_call" | custom-call | flops 1000000 | bytes 2000000 | tf_op jit(solution)/shard_map/pack_y/pallas_call | solution.py:207
  13.5 0.0 collective-permute-done.x_near
  13.6 1.5 %collective-permute-done.1.x_far = f32[264,128]{1,0:T(8,128)S(1)} collective-permute-done((f32[264,128]{1,0:T(8,128)}, f32[264,128]{1,0:T(8,128)S(1)}, u32[]{:S(2)}, u32[]{:S(2)}) %collective-permute-start.1) | collective-permute-done | bytes 135200 | tf_op jit(solution)/shard_map/ppermute | solution.py:658
  15.1 0.1 add_edges.1
  15.2 0.9 %collective-permute-start.2 = (f32[200,128]{1,0:T(8,128)S(1)}, f32[200,128]{1,0:T(8,128)S(1)}, u32[]{:S(2)}, u32[]{:S(2)}) collective-permute-start(f32[200,128]{1,0:T(8,128)S(1)} %get-tuple-element.14), channel_id=1, source_target_pairs={{0,1},{1,0},{2,3},{3,2},{4,5},{5,4},{6,7},{7,6},{8,9},{9,8},{10,11... | collective-permute-start | bytes 307208 | tf_op jit(solution)/shard_map/ppermute | solution.py:658
  16.1 0.0 copy-start.1
  16.1 0.0 copy-start.4
  16.1 0.8 %collective-permute-start.3 = (f32[200,128]{1,0:T(8,128)S(1)}, f32[200,128]{1,0:T(8,128)S(1)}, u32[]{:S(2)}, u32[]{:S(2)}) collective-permute-start(f32[200,128]{1,0:T(8,128)S(1)} %get-tuple-element.15), channel_id=1, source_target_pairs={{0,7},{1,2},{2,1},{3,4},{4,3},{5,6},{6,5},{7,0},{8,15},{9,10},{10,... | collective-permute-start | bytes 307208 | tf_op jit(solution)/shard_map/ppermute | solution.py:658
  16.9 0.0 copy-done.3
  16.9 4.0 %spread_own.1.own_force = f32[4,512,128]{2,1,0:T(8,128)S(1)} custom-call(s32[1,1,8]{2,1,0:T(1,128)S(1)} %copy-done.6, s32[1,1,8,20]{3,2,1,0:T(8,128)S(1)} %copy-done.5, f32[1,1,9,8,1280]{4,3,2,1,0:T(8,128)S(1)} %bitcast.8, bf16[1280,1280]{1,0:T(8,128)(2,1)S(1)} %copy-done.3), custom_call_target="tpu_custom_call" | custom-call | flops 2000000000 | bytes 5000000 | tf_op jit(solution)/shard_map/spread_own/pallas_call | solution.py:362
  20.9 0.0 collective-permute-done.2.y_near
  20.9 1.9 %collective-permute-done.3.y_far = f32[200,128]{1,0:T(8,128)S(1)} collective-permute-done((f32[200,128]{1,0:T(8,128)S(1)}, f32[200,128]{1,0:T(8,128)S(1)}, u32[]{:S(2)}, u32[]{:S(2)}) %collective-permute-start.3) | collective-permute-done | bytes 102432 | tf_op jit(solution)/shard_map/ppermute | solution.py:658
  22.9 0.0 copy-done.1
  22.9 0.0 copy-done.4
  22.9 9.5 %lattice_step.1 = (f32[19,256,128]{2,1,0:T(8,128)}, f32[1,1,9,16,1280]{4,3,2,1,0:T(8,128)}) custom-call(s32[1,1,8]{2,1,0:T(1,128)S(1)} %copy-done.6, s32[1,1,8,20]{3,2,1,0:T(8,128)S(1)} %copy-done.5, f32[19,256,128]{2,1,0:T(8,128)S(1)} %bitcast.5, s32[256,128]{1,0:T(8,128)S(1)} %bitcast.10, f32[1,1,9,8,1280]{4,3,2,1,0:T(8,128)S(1)} %bitcast.9, ...), custom_call_target="tpu_custom_call" | custom-call | flops 2000000000 | bytes 10000000 | tf_op jit(solution)/shard_map/lattice_step/pallas_call | solution.py:619
Async XLA Ops:
  0.6 10.0 %copy-start.6 = (s32[1,1,8]{2,1,0:T(1,128)S(1)}, s32[1,1,8]{2,1,0:T(1,128)}, u32[]{:S(2)}) copy-start(s32[1,1,8]{2,1,0:T(1,128)} %leave_hbm.7) | copy-start | bytes 100
  0.6 10.0 %copy-start.5 = (s32[1,1,8,20]{3,2,1,0:T(8,128)S(1)}, s32[1,1,8,20]{3,2,1,0:T(8,128)}, u32[]{:S(2)}) copy-start(s32[1,1,8,20]{3,2,1,0:T(8,128)} %bricks_hbm.7) | copy-start | bytes 1924
  0.7 10.0 %copy-start.2 = (f32[1,1,8,9,1280]{4,2,3,1,0:T(8,128)S(1)}, f32[1,1,8,9,1280]{4,2,3,1,0:T(8,128)}, u32[]{:S(2)}) copy-start(f32[1,1,8,9,1280]{4,2,3,1,0:T(8,128)} %param.8) | copy-start | bytes 1105924
  2.8 10.7 %collective-permute-start = (f32[264,128]{1,0:T(8,128)}, f32[264,128]{1,0:T(8,128)S(1)}, u32[]{:S(2)}, u32[]{:S(2)}) collective-permute-start(f32[264,128]{1,0:T(8,128)} %get-tuple-element.10), channel_id=1, source_target_pairs={{0,8},{8,0},{16,24},{24,16},{32,40},{40,32},{48,56},{56,48},{64,72... | collective-permute-start | bytes 405512 | tf_op jit(solution)/shard_map/ppermute | solution.py:658
  2.9 12.2 %collective-permute-start.1 = (f32[264,128]{1,0:T(8,128)}, f32[264,128]{1,0:T(8,128)S(1)}, u32[]{:S(2)}, u32[]{:S(2)}) collective-permute-start(f32[264,128]{1,0:T(8,128)} %get-tuple-element.11), channel_id=1, source_target_pairs={{0,248},{8,16},{16,8},{24,32},{32,24},{40,48},{48,40},{56,64},{64,... | collective-permute-start | bytes 405512 | tf_op jit(solution)/shard_map/ppermute | solution.py:658
  10.6 1.7 %copy-start = (f32[19,16,16,128]{3,2,1,0:T(8,128)S(1)}, f32[19,16,16,128]{3,2,1,0:T(8,128)}, u32[]{:S(2)}) copy-start(f32[19,16,16,128]{3,2,1,0:T(8,128)} %pops_hbm.3) | copy-start | bytes 7471108
  12.3 4.6 %copy-start.3 = (bf16[1280,1280]{1,0:T(8,128)(2,1)S(1)}, bf16[1280,1280]{1,0:T(8,128)(2,1)}, u32[]{:S(2)}) copy-start(bf16[1280,1280]{1,0:T(8,128)(2,1)} %stiffness.3) | copy-start | bytes 9830404
  15.2 5.7 %collective-permute-start.2 = (f32[200,128]{1,0:T(8,128)S(1)}, f32[200,128]{1,0:T(8,128)S(1)}, u32[]{:S(2)}, u32[]{:S(2)}) collective-permute-start(f32[200,128]{1,0:T(8,128)S(1)} %get-tuple-element.14), channel_id=1, source_target_pairs={{0,1},{1,0},{2,3},{3,2},{4,5},{5,4},{6,7},{7,6},{8,9},{9,8},{10,11... | collective-permute-start | bytes 307208 | tf_op jit(solution)/shard_map/ppermute | solution.py:658
  16.1 6.8 %copy-start.1 = (f32[19,16,16,128]{3,2,1,0:T(8,128)S(1)}, f32[19,16,16,128]{3,2,1,0:T(8,128)}, u32[]{:S(2)}) copy-start(f32[19,16,16,128]{3,2,1,0:T(8,128)} %pops_hbm.3) | copy-start | bytes 7471108
  16.1 6.8 %copy-start.4 = (s32[16,16,128]{2,1,0:T(8,128)S(1)}, s32[16,16,128]{2,1,0:T(8,128)}, u32[]{:S(2)}) copy-start(s32[16,16,128]{2,1,0:T(8,128)} %param.7) | copy-start | bytes 393220
  16.1 6.8 %collective-permute-start.3 = (f32[200,128]{1,0:T(8,128)S(1)}, f32[200,128]{1,0:T(8,128)S(1)}, u32[]{:S(2)}, u32[]{:S(2)}) collective-permute-start(f32[200,128]{1,0:T(8,128)S(1)} %get-tuple-element.15), channel_id=1, source_target_pairs={{0,7},{1,2},{2,1},{3,4},{4,3},{5,6},{6,5},{7,0},{8,15},{9,10},{10,... | collective-permute-start | bytes 307208 | tf_op jit(solution)/shard_map/ppermute | solution.py:658

commit v4 on v3

--- a/solution.py
+++ b/solution.py
@@ -464,6 +464,7 @@
             flow[4 + k, at, :] = momentum[k] * inverse
         return carry
 
+    stiff_product(push, guests, stiffness)
     lax.fori_loop(0, NZ, pull, 0, unroll=True)
 
     left = lanes((16, 128)) < 64
@@ -486,7 +487,6 @@
                     base = (bz * 2 + bx) * 16 * 8
                     cells[j, pl.ds(base + k, 16, stride=8), :] = pairs[bx]
 
-    stiff_product(push, guests, stiffness)
     force[...] = jnp.zeros(force.shape, F32)
     speeds[...] = jnp.zeros(speeds.shape, F32)
     for copy in copies:

time: 32.1 us -> 32.3 us (level); the launches traced: 32.4 us -> 32 us
  Pallas kernels: 17 us -> 16 us
  waiting for transfers between devices: 3.49 us -> 4.03 us
    pallas_call x1, Pallas kernels: 3.99 us -> 3.45 us  [spread_own(): pl.pallas_call(own_kernel, out_shape=jax.ShapeDtypeStruct((4, 512, 128),...]
    ppermute x4, waiting for transfers between devices: 3.49 us -> 4.03 us  [exchange(): lax.ppermute(x, axis, [(i, (i + (1 if i % 2 == far else -1)) % size) for...]
    pallas_call x1, Pallas kernels: 9.53 us -> 9.12 us  [step(): pl.pallas_call(step_kernel, out_shape=[jax.ShapeDtypeStruct((19, NZ * CX,...]
  transfers between devices with their start and end apart: 4 -> 4, of which waited for: 2 -> 2; matrix products, arithmetic and copies ran while one was open for 0% -> 0% of each run, Pallas kernels for 16% -> 15%
where the time goes in v4:
time: 32.3 us; the launch traced here: 32 us
  Pallas kernels  16 us (50%)
  starting transfers between devices  9.5 us (29%)
  waiting for transfers between devices  4.03 us (12%)
  local copies, waits for them, and re-layouts  1.72 us (5%)
  between operations  0.72 us (2%)
    ppermute x4, starting transfers between devices, exchange(): lax.ppermute(x, axis, [(i, (i + (1 if i % 2 == far else -1)) % size) for...  9.5 us
    pallas_call x1, Pallas kernels, step(): pl.pallas_call(step_kernel, out_shape=[jax.ShapeDtypeStruct((19, NZ * CX,...  9.12 us
    ppermute x4, waiting for transfers between devices, exchange(): lax.ppermute(x, axis, [(i, (i + (1 if i % 2 == far else -1)) % size) for...  4.03 us
    pallas_call x1, Pallas kernels, spread_own(): pl.pallas_call(own_kernel, out_shape=jax.ShapeDtypeStruct((4, 512, 128),...  3.45 us
    pallas_call x1, Pallas kernels, pack_x(): pl.pallas_call(pack_x_kernel, out_shape=[jax.ShapeDtypeStruct((X_ROWS, 12...  2.17 us
    unnamed x14, local copies, waits for them, and re-layouts  1.72 us
    pallas_call x1, Pallas kernels, pack_y(): pl.pallas_call(pack_y_kernel, out_shape=[jax.ShapeDtypeStruct((Y_ROWS, 12...  1.19 us
  transfers between devices with their start and end apart: 4, of which 2 were waited for; matrix products, arithmetic and copies ran while one was open for 0% of the time, Pallas kernels for 15%

profile of v4, /device:TPU:56, one launch (start us, length us, event | category | flops | bytes accessed | tf_op | source)
XLA Modules:
  0.0 32.0 jit_solution(1270858802512139250)
XLA Ops:
  0.6 0.0 copy-start.6
  0.6 0.0 copy-start.5
  0.7 0.0 copy-start.2
  0.7 2.2 %pack_x.1 = (f32[264,128]{1,0:T(8,128)}, f32[264,128]{1,0:T(8,128)}) custom-call(s32[1,1,8]{2,1,0:T(1,128)} %leave_hbm.7, s32[1,1,8,20]{3,2,1,0:T(8,128)} %bricks_hbm.7, f32[1,1,9,8,1280]{4,3,2,1,0:T(8,128)} %bitcast.6, f32[19,16,16,128]{3,2,1,0:T(8,128)} %pops_hbm.3), custom_call_target="tpu_custom_call" | custom-call | flops 1000000 | bytes 1000000 | tf_op jit(solution)/shard_map/pack_x/pallas_call | solution.py:193
  2.8 0.1 collective-permute-start
  2.9 7.7 %collective-permute-start.1 = (f32[264,128]{1,0:T(8,128)}, f32[264,128]{1,0:T(8,128)S(1)}, u32[]{:S(2)}, u32[]{:S(2)}) collective-permute-start(f32[264,128]{1,0:T(8,128)} %get-tuple-element.11), channel_id=1, source_target_pairs={{0,248},{8,16},{16,8},{24,32},{32,24},{40,48},{48,40},{56,64},{64,... | collective-permute-start | bytes 405512 | tf_op jit(solution)/shard_map/ppermute | solution.py:658
  10.6 0.0 copy-done.6
  10.6 0.0 copy-done.5
  10.6 0.0 copy-done.2
  10.6 0.0 copy-start
  10.6 1.7 %copy-done = f32[19,16,16,128]{3,2,1,0:T(8,128)S(1)} copy-done((f32[19,16,16,128]{3,2,1,0:T(8,128)S(1)}, f32[19,16,16,128]{3,2,1,0:T(8,128)}, u32[]{:S(2)}) %copy-start) | copy-done | bytes 2490392
  12.3 0.0 copy-start.3
  12.3 1.2 %pack_y.1 = (f32[200,128]{1,0:T(8,128)S(1)}, f32[200,128]{1,0:T(8,128)S(1)}) custom-call(s32[1,1,8]{2,1,0:T(1,128)S(1)} %copy-done.6, s32[1,1,8,20]{3,2,1,0:T(8,128)S(1)} %copy-done.5, f32[1,1,9,8,1280]{4,3,2,1,0:T(8,128)S(1)} %bitcast.7, f32[19,16,16,128]{3,2,1,0:T(8,128)S(1)} %copy-done), custom_call_target="tpu_custom_call" | custom-call | flops 1000000 | bytes 2000000 | tf_op jit(solution)/shard_map/pack_y/pallas_call | solution.py:207
  13.5 0.0 collective-permute-done.x_near
  13.6 1.5 %collective-permute-done.1.x_far = f32[264,128]{1,0:T(8,128)S(1)} collective-permute-done((f32[264,128]{1,0:T(8,128)}, f32[264,128]{1,0:T(8,128)S(1)}, u32[]{:S(2)}, u32[]{:S(2)}) %collective-permute-start.1) | collective-permute-done | bytes 135200 | tf_op jit(solution)/shard_map/ppermute | solution.py:658
  15.1 0.1 add_edges.1
  15.2 0.9 %collective-permute-start.2 = (f32[200,128]{1,0:T(8,128)S(1)}, f32[200,128]{1,0:T(8,128)S(1)}, u32[]{:S(2)}, u32[]{:S(2)}) collective-permute-start(f32[200,128]{1,0:T(8,128)S(1)} %get-tuple-element.14), channel_id=1, source_target_pairs={{0,1},{1,0},{2,3},{3,2},{4,5},{5,4},{6,7},{7,6},{8,9},{9,8},{10,11... | collective-permute-start | bytes 307208 | tf_op jit(solution)/shard_map/ppermute | solution.py:658
  16.1 0.0 copy-start.1
  16.1 0.0 copy-start.4
  16.1 0.8 %collective-permute-start.3 = (f32[200,128]{1,0:T(8,128)S(1)}, f32[200,128]{1,0:T(8,128)S(1)}, u32[]{:S(2)}, u32[]{:S(2)}) collective-permute-start(f32[200,128]{1,0:T(8,128)S(1)} %get-tuple-element.15), channel_id=1, source_target_pairs={{0,7},{1,2},{2,1},{3,4},{4,3},{5,6},{6,5},{7,0},{8,15},{9,10},{10,... | collective-permute-start | bytes 307208 | tf_op jit(solution)/shard_map/ppermute | solution.py:658
  16.9 0.0 copy-done.3
  16.9 3.5 %spread_own.1.own_force = f32[4,512,128]{2,1,0:T(8,128)S(1)} custom-call(s32[1,1,8]{2,1,0:T(1,128)S(1)} %copy-done.6, s32[1,1,8,20]{3,2,1,0:T(8,128)S(1)} %copy-done.5, f32[1,1,9,8,1280]{4,3,2,1,0:T(8,128)S(1)} %bitcast.8, bf16[1280,1280]{1,0:T(8,128)(2,1)S(1)} %copy-done.3), custom_call_target="tpu_custom_call" | custom-call | flops 2000000000 | bytes 5000000 | tf_op jit(solution)/shard_map/spread_own/pallas_call | solution.py:362
  20.4 0.0 collective-permute-done.2.y_near
  20.4 2.5 %collective-permute-done.3.y_far = f32[200,128]{1,0:T(8,128)S(1)} collective-permute-done((f32[200,128]{1,0:T(8,128)S(1)}, f32[200,128]{1,0:T(8,128)S(1)}, u32[]{:S(2)}, u32[]{:S(2)}) %collective-permute-start.3) | collective-permute-done | bytes 102432 | tf_op jit(solution)/shard_map/ppermute | solution.py:658
  22.9 0.0 copy-done.1
  22.9 0.0 copy-done.4
  22.9 9.1 %lattice_step.1 = (f32[19,256,128]{2,1,0:T(8,128)}, f32[1,1,9,16,1280]{4,3,2,1,0:T(8,128)}) custom-call(s32[1,1,8]{2,1,0:T(1,128)S(1)} %copy-done.6, s32[1,1,8,20]{3,2,1,0:T(8,128)S(1)} %copy-done.5, f32[19,256,128]{2,1,0:T(8,128)S(1)} %bitcast.5, s32[256,128]{1,0:T(8,128)S(1)} %bitcast.10, f32[1,1,9,8,1280]{4,3,2,1,0:T(8,128)S(1)} %bitcast.9, ...), custom_call_target="tpu_custom_call" | custom-call | flops 2000000000 | bytes 10000000 | tf_op jit(solution)/shard_map/lattice_step/pallas_call | solution.py:619
Async XLA Ops:
  0.6 10.0 %copy-start.6 = (s32[1,1,8]{2,1,0:T(1,128)S(1)}, s32[1,1,8]{2,1,0:T(1,128)}, u32[]{:S(2)}) copy-start(s32[1,1,8]{2,1,0:T(1,128)} %leave_hbm.7) | copy-start | bytes 100
  0.6 10.0 %copy-start.5 = (s32[1,1,8,20]{3,2,1,0:T(8,128)S(1)}, s32[1,1,8,20]{3,2,1,0:T(8,128)}, u32[]{:S(2)}) copy-start(s32[1,1,8,20]{3,2,1,0:T(8,128)} %bricks_hbm.7) | copy-start | bytes 1924
  0.7 10.0 %copy-start.2 = (f32[1,1,8,9,1280]{4,2,3,1,0:T(8,128)S(1)}, f32[1,1,8,9,1280]{4,2,3,1,0:T(8,128)}, u32[]{:S(2)}) copy-start(f32[1,1,8,9,1280]{4,2,3,1,0:T(8,128)} %param.8) | copy-start | bytes 1105924
  2.8 10.7 %collective-permute-start = (f32[264,128]{1,0:T(8,128)}, f32[264,128]{1,0:T(8,128)S(1)}, u32[]{:S(2)}, u32[]{:S(2)}) collective-permute-start(f32[264,128]{1,0:T(8,128)} %get-tuple-element.10), channel_id=1, source_target_pairs={{0,8},{8,0},{16,24},{24,16},{32,40},{40,32},{48,56},{56,48},{64,72... | collective-permute-start | bytes 405512 | tf_op jit(solution)/shard_map/ppermute | solution.py:658
  2.9 12.2 %collective-permute-start.1 = (f32[264,128]{1,0:T(8,128)}, f32[264,128]{1,0:T(8,128)S(1)}, u32[]{:S(2)}, u32[]{:S(2)}) collective-permute-start(f32[264,128]{1,0:T(8,128)} %get-tuple-element.11), channel_id=1, source_target_pairs={{0,248},{8,16},{16,8},{24,32},{32,24},{40,48},{48,40},{56,64},{64,... | collective-permute-start | bytes 405512 | tf_op jit(solution)/shard_map/ppermute | solution.py:658
  10.6 1.7 %copy-start = (f32[19,16,16,128]{3,2,1,0:T(8,128)S(1)}, f32[19,16,16,128]{3,2,1,0:T(8,128)}, u32[]{:S(2)}) copy-start(f32[19,16,16,128]{3,2,1,0:T(8,128)} %pops_hbm.3) | copy-start | bytes 7471108
  12.3 4.6 %copy-start.3 = (bf16[1280,1280]{1,0:T(8,128)(2,1)S(1)}, bf16[1280,1280]{1,0:T(8,128)(2,1)}, u32[]{:S(2)}) copy-start(bf16[1280,1280]{1,0:T(8,128)(2,1)} %stiffness.3) | copy-start | bytes 9830404
  15.2 5.2 %collective-permute-start.2 = (f32[200,128]{1,0:T(8,128)S(1)}, f32[200,128]{1,0:T(8,128)S(1)}, u32[]{:S(2)}, u32[]{:S(2)}) collective-permute-start(f32[200,128]{1,0:T(8,128)S(1)} %get-tuple-element.14), channel_id=1, source_target_pairs={{0,1},{1,0},{2,3},{3,2},{4,5},{5,4},{6,7},{7,6},{8,9},{9,8},{10,11... | collective-permute-start | bytes 307208 | tf_op jit(solution)/shard_map/ppermute | solution.py:658
  16.1 6.8 %copy-start.1 = (f32[19,16,16,128]{3,2,1,0:T(8,128)S(1)}, f32[19,16,16,128]{3,2,1,0:T(8,128)}, u32[]{:S(2)}) copy-start(f32[19,16,16,128]{3,2,1,0:T(8,128)} %pops_hbm.3) | copy-start | bytes 7471108
  16.1 6.8 %copy-start.4 = (s32[16,16,128]{2,1,0:T(8,128)S(1)}, s32[16,16,128]{2,1,0:T(8,128)}, u32[]{:S(2)}) copy-start(s32[16,16,128]{2,1,0:T(8,128)} %param.7) | copy-start | bytes 393220
  16.1 6.8 %collective-permute-start.3 = (f32[200,128]{1,0:T(8,128)S(1)}, f32[200,128]{1,0:T(8,128)S(1)}, u32[]{:S(2)}, u32[]{:S(2)}) collective-permute-start(f32[200,128]{1,0:T(8,128)S(1)} %get-tuple-element.15), channel_id=1, source_target_pairs={{0,7},{1,2},{2,1},{3,4},{4,3},{5,6},{6,5},{7,0},{8,15},{9,10},{10,... | collective-permute-start | bytes 307208 | tf_op jit(solution)/shard_map/ppermute | solution.py:658
